TPU v7x, 32 devices: a whole 2x2x4 slice. The times are simulated.
32 devices in a mesh: dp: 32 (over z, y, x, core).
Axes of the slice: x: 2, y: 2, z: 4, core: 2. Of those that a mesh axis runs over, the one named last changes fastest.
Arguments:
- grads: bfloat16 [64, 1024, 1024], P('dp'), may hold values from -6 to 6
- memory: bfloat16 [64, 1024, 1024], P('dp'), may hold values from -6 to 6
- block_ids: int32 [16], replicated, may hold values from 0 to 63, as said below
- layer_ids: int32 [16], replicated, may hold values from 0 to 1, as said below
- master: float32 [128, 16384], P(None, 'dp'), may hold values from -8 to 8
- first_moment: float32 [128, 16384], P(None, 'dp'), may hold values from -8 to 8
- second_moment: float32 [128, 16384], P(None, 'dp'), may hold values from 0.25 to 4
Outputs:
- new_memory: bfloat16 [64, 1024, 1024], P('dp')
- master_new: float32 [128, 16384], P(None, 'dp')
- first_new: float32 [128, 16384], P(None, 'dp')
- second_new: float32 [128, 16384], P(None, 'dp')
- step_blocks: bfloat16 [16, 16384], replicated
Inputs may be any that keep to these rules, and one draw needn't show every extreme that they name: Block ids number the 64 tiles of a layer, and the pairs (layer_ids[k], block_ids[k]) are distinct. `layer_ids`: every layer is named by at least a quarter of the 16 entries, rounded down.
All inputs are finite; a program needn't handle non-finite values.
Results may differ from a plain program's by a relative error of at most 0.0004.
Values may be sent and summed in bfloat16 or wider, within the bound.
A program may use at most 64 MiB of HBM per device.

v0:
```python
import jax
import jax.numpy as jnp
from jax import lax
from jax.sharding import PartitionSpec as P

TILE = 128


filter_rate = 0.3
beta_one = 0.9
beta_two = 0.999
adam_eps = 1e-06
weight_decay = 0.01
learn_rate = 0.01
norm_eps = 1e-06


def take_tiles(source, layer_ids, tile_row, tile_col):

    def single(layer_id, row_tile, col_tile):
        return lax.dynamic_slice(
            source, (layer_id, row_tile * TILE, col_tile * TILE), (1, TILE, TILE)
        )[0]

    return jax.vmap(single)(layer_ids, tile_row, tile_col)


def pack_blocks(grads_dev, memory_dev, layer_ids, tile_row, tile_col):
    grad_tiles = take_tiles(grads_dev, layer_ids, tile_row, tile_col).astype(jnp.float32)
    memory_tiles = take_tiles(memory_dev, layer_ids, tile_row, tile_col).astype(jnp.float32)
    combined = grad_tiles + memory_tiles
    return combined.reshape(combined.shape[0], TILE * TILE)


def selected_mask(layer_ids, block_ids, layers, tile_count):
    columns = layer_ids * (tile_count * tile_count) + block_ids
    all_columns = jnp.arange(layers * tile_count * tile_count, dtype=jnp.int32)
    chosen = jnp.any(columns[:, None] == all_columns[None, :], axis=0)
    return chosen.reshape(layers, tile_count, 1, tile_count, 1)


def filter_memory(grads_dev, memory_dev, chosen):
    layers, model_width, _ = grads_dev.shape
    tile_count = model_width // TILE
    accumulated = grads_dev.astype(jnp.float32) + memory_dev.astype(jnp.float32)
    shaped = accumulated.reshape(layers, tile_count, TILE, tile_count, TILE)
    filtered = jnp.where(chosen, jnp.float32(0.0), shaped).reshape(layers, model_width, model_width)
    mixed = (1.0 - filter_rate) * memory_dev.astype(jnp.float32) + filter_rate * filtered
    return mixed.astype(jnp.bfloat16)


def adam_rows(summed, weights_sel, first_old, second_old):
    first_sel = beta_one * first_old + (1.0 - beta_one) * summed
    second_sel = beta_two * second_old + (1.0 - beta_two) * summed * summed
    update = first_sel / (jnp.sqrt(second_sel) + adam_eps) + weight_decay * weights_sel
    return (first_sel, second_sel, update)


def layer_squares(member, values):
    return jnp.sum(member * jnp.sum(values * values, axis=1)[:, None], axis=0)


def trust_rows(member, weight_total, update_total):
    trust_ratio = jnp.sqrt(weight_total / (update_total + norm_eps))
    return jnp.sum(member * trust_ratio[None, :], axis=1)


def on_device(grads, memory, block_ids, layer_ids, master, first_moment, second_moment):
    layers, model_width, _ = grads.shape
    tile_count = model_width // TILE
    tile_row = block_ids // tile_count
    tile_col = block_ids % tile_count
    columns = layer_ids * (tile_count * tile_count) + block_ids
    member = (layer_ids[:, None] == jnp.arange(layers, dtype=jnp.int32)[None, :]).astype(
        jnp.float32
    )
    weights_sel = jnp.take(master, columns, axis=0)
    first_old = jnp.take(first_moment, columns, axis=0)
    second_old = jnp.take(second_moment, columns, axis=0)
    packed = pack_blocks(grads, memory, layer_ids, tile_row, tile_col)
    summed = lax.psum_scatter(packed, "dp", scatter_dimension=1, tiled=True)
    first_sel, second_sel, update = adam_rows(summed, weights_sel, first_old, second_old)
    weight_total, update_total = lax.psum(
        (layer_squares(member, weights_sel), layer_squares(member, update)), "dp"
    )
    scaled = trust_rows(member, weight_total, update_total)[:, None] * update
    step_blocks = lax.all_gather(scaled.astype(jnp.bfloat16), "dp", axis=1, tiled=True)
    new_memory = filter_memory(
        grads, memory, selected_mask(layer_ids, block_ids, layers, tile_count)
    )
    master_new = master.at[columns].set(weights_sel - learn_rate * scaled)
    first_new = first_moment.at[columns].set(first_sel)
    second_new = second_moment.at[columns].set(second_sel)
    return (new_memory, master_new, first_new, second_new, step_blocks)


def solution(mesh):
    in_specs = (
        P("dp", None, None),
        P("dp", None, None),
        P(),
        P(),
        P(None, "dp"),
        P(None, "dp"),
        P(None, "dp"),
    )
    out_specs = (P("dp", None, None), P(None, "dp"), P(None, "dp"), P(None, "dp"), P())
    return jax.shard_map(
        on_device, mesh=mesh, in_specs=in_specs, out_specs=out_specs, check_vma=False
    )
```

profile of v0, /device:TPU:0, one launch (start us, length us, event | category | flops | bytes accessed | tf_op | source)
XLA Modules:
  0.0 355.2 jit_solution(294397355076881631)
XLA Ops:
  7.2 1.0 copy.36
  8.2 1.0 copy.38
  9.1 0.9 copy.37
  10.1 0.7 fusion.20
  10.9 56.4 %while.3 = (s32[]{:T(128)}, bf16[2,1024,1024]{2,1,0:T(8,128)(2,1)}, s32[16,3]{0,1:T(4,128)S(1)}, bf16[16,1,128,128]{3,2,1,0:T(8,128)(2,1)S(1)}, s32[]{:T(128)}) while((s32[]{:T(128)}, bf16[2,1024,1024]{2,1,0:T(8,128)(2,1)}, s32[16,3]{0,1:T(4,128)S(1)}, bf16[16,1,128,128]{3,2,1,0:T(8,128)(2,1)S(1)}, s32[]{:T(128)}) %tuple.46), condition=%wide.while_cond.1, body=%wide.while_body.1.sunk | while | flops 2 | bytes 65673 | solution.py:21
  11.5 2.9 bitcast_dynamic-update-slice_fusion.5
  15.1 2.9 bitcast_dynamic-update-slice_fusion.5
  18.0 0.5 fusion.30
  18.6 2.9 bitcast_dynamic-update-slice_fusion.5
  21.6 0.5 fusion.30
  22.1 2.9 bitcast_dynamic-update-slice_fusion.5
  25.1 0.5 fusion.30
  25.7 2.9 bitcast_dynamic-update-slice_fusion.5
  28.7 0.5 fusion.30
  29.2 2.9 bitcast_dynamic-update-slice_fusion.5
  32.2 0.5 fusion.30
  32.7 2.9 bitcast_dynamic-update-slice_fusion.5
  36.3 2.9 bitcast_dynamic-update-slice_fusion.5
  39.8 2.9 bitcast_dynamic-update-slice_fusion.5
  43.4 2.8 bitcast_dynamic-update-slice_fusion.5
  46.3 0.5 fusion.30
  46.8 2.9 bitcast_dynamic-update-slice_fusion.5
  49.8 0.5 fusion.30
  50.3 2.9 bitcast_dynamic-update-slice_fusion.5
  53.9 2.8 bitcast_dynamic-update-slice_fusion.5
  57.3 2.9 bitcast_dynamic-update-slice_fusion.5
  60.3 0.5 fusion.30
  60.8 2.9 bitcast_dynamic-update-slice_fusion.5
  63.9 0.5 fusion.30
  64.4 2.9 bitcast_dynamic-update-slice_fusion.5
  67.4 56.4 %while.2 = (s32[]{:T(128)}, bf16[2,1024,1024]{2,1,0:T(8,128)(2,1)}, s32[16,3]{0,1:T(4,128)S(1)}, bf16[16,1,128,128]{3,2,1,0:T(8,128)(2,1)S(1)}, s32[]{:T(128)}) while((s32[]{:T(128)}, bf16[2,1024,1024]{2,1,0:T(8,128)(2,1)}, s32[16,3]{0,1:T(4,128)S(1)}, bf16[16,1,128,128]{3,2,1,0:T(8,128)(2,1)S(1)}, s32[]{:T(128)}) %tuple.56), condition=%wide.while_cond, body=%wide.while_body.sunk | while | flops 2 | bytes 65673 | solution.py:21
  67.5 0.5 fusion.29
  68.0 2.9 bitcast_dynamic-update-slice_fusion.4
  71.1 0.5 fusion.29
  71.6 2.9 bitcast_dynamic-update-slice_fusion.4
  75.1 2.9 bitcast_dynamic-update-slice_fusion.4
  78.6 2.9 bitcast_dynamic-update-slice_fusion.4
  82.2 2.9 bitcast_dynamic-update-slice_fusion.4
  85.7 2.9 bitcast_dynamic-update-slice_fusion.4
  89.3 2.9 bitcast_dynamic-update-slice_fusion.4
  92.8 2.9 bitcast_dynamic-update-slice_fusion.4
  96.4 2.9 bitcast_dynamic-update-slice_fusion.4
  99.9 2.8 bitcast_dynamic-update-slice_fusion.4
  103.4 2.9 bitcast_dynamic-update-slice_fusion.4
  106.9 2.9 bitcast_dynamic-update-slice_fusion.4
  110.4 2.8 bitcast_dynamic-update-slice_fusion.4
  113.8 2.9 bitcast_dynamic-update-slice_fusion.4
  117.4 2.9 bitcast_dynamic-update-slice_fusion.4
  120.9 2.9 bitcast_dynamic-update-slice_fusion.4
  124.0 1.6 copy.14
  125.8 1.9 broadcast_in_dim.51
  127.8 5.3 %broadcast_in_dim.52 = pred[2,1024,1024]{2,1,0:T(8,128)(4,1)S(1)} reshape(pred[2,8,128,8,128]{4,3,2,1,0:T(8,128)(4,1)} %broadcast_in_dim.51) | data formatting | bytes 4194304 | tf_op jit(solution)/shard_map/jit(_where)/broadcast_in_dim | solution.py:47
  133.1 0.6 gather_fusion
  133.7 0.6 gather_fusion.2
  134.2 0.6 gather_fusion.1
  134.8 6.2 %fusion.1 = bf16[2,1024,1024]{2,1,0:T(8,128)(2,1)} fusion(bf16[2,1024,1024]{2,1,0:T(8,128)(2,1)} %get-tuple-element.159, pred[2,1024,1024]{2,1,0:T(8,128)(4,1)S(1)} %broadcast_in_dim.52, bf16[2,1024,1024]{2,1,0:T(8,128)(2,1)} %get-tuple-element.160), kind=kLoop, calls=%fused_computation.13 | loop fusion | flops 16777216 | bytes 14680064 | tf_op jit(solution)/shard_map/convert_element_type | solution.py:49
  141.1 124.0 %reduce-scatter.2.cloned.1.call-done = f32[16,512]{1,0:T(8,128)} async-done(((f32[16,16384]{1,0:T(8,128)}), f32[16,512]{1,0:T(8,128)}) %reduce-scatter.2.cloned.1.call-update) | async-done | bytes 32784 | tf_op jit(solution)/shard_map/reduce_scatter | solution.py:81
  265.0 1.0 multiply_reduce_fusion
  266.1 36.9 %all-reduce = (f32[2]{0:T(128)S(1)}, f32[2]{0:T(128)S(1)}) all-reduce(f32[2]{0:T(128)S(1)} %get-tuple-element.23, f32[2]{0:T(128)S(1)} %get-tuple-element.22), channel_id=1, replica_groups=mesh['dp'=32] {'dp'}, use_global_device_ids=true, to_apply=%region_3.5 | all-reduce | flops 4 | bytes 32 | tf_op jit(solution)/shard_map/psum | solution.py:83
  303.2 41.3 %all_gather.3 = bf16[16,16384]{1,0:T(8,128)(2,1)S(1)} all-gather(bf16[16,512]{1,0:T(8,128)(2,1)S(1)} %multiply_convert_fusion), channel_id=1, replica_groups=mesh['dp'=32] {'dp'}, dimensions={1}, use_global_device_ids=true | all-gather | bytes 540672 | tf_op jit(solution)/shard_map/all_gather | solution.py:87
  344.4 0.8 scatter_custom_fusion
  345.3 1.1 scatter_custom_fusion.1
  346.4 1.1 scatter_custom_fusion.2
  347.5 0.8 copy.40
  (78 shorter events, 14.3 us)
Async XLA Ops:
  7.2 257.8 %reduce-scatter.2.cloned.1.call-start = ((), (), s32[]{:S(2)}) async-start(), calls=%async_computation.1 | async-start | bytes 1081344 | tf_op jit(solution)/shard_map/reduce_scatter | solution.py:81
  8.2 117.5 %copy-start.3 = (s32[16]{0:T(128)S(1)}, s32[16]{0:T(128)}, u32[]{:S(2)}) copy-start(s32[16]{0:T(128)} %param.12) | copy-start | bytes 196
  8.2 117.5 %copy-start.4 = (s32[16]{0:T(128)S(1)}, s32[16]{0:T(128)}, u32[]{:S(2)}) copy-start(s32[16]{0:T(128)} %param.11) | copy-start | bytes 196
  345.3 3.1 copy-start.2
  346.4 2.0 copy-start.1
  347.5 0.9 copy-start
Sparse Core Ops, SparseCore 0:
  125.7 139.2 reduce-scatter.1
where the time goes:
time: 358 us; the launch traced here: 355 us
  local copies, waits for them, and re-layouts  127 us (35%)
  waiting for transfers between devices  124 us (35%)
  blocking collectives  78.1 us (22%)
  between operations  14.2 us (4%)
  other arithmetic  11.5 us (3%)
    reduce_scatter x1, waiting for transfers between devices, on_device(): summed = lax.psum_scatter(packed, 'dp', scatter_dimension=1, tiled=True)  124 us
    gather x96, local copies, waits for them, and re-layouts  112 us
    all_gather x1, blocking collectives, on_device(): lax.all_gather(scaled.astype(jnp.bfloat16), 'dp', axis=1, tiled=True)  41.3 us
    psum x1, blocking collectives, on_device(): lax.psum((layer_squares(member, weights_sel), layer_squares(member, updat...  36.9 us
    broadcast_in_dim x3, local copies, waits for them, and re-layouts, filter_memory(): jnp.where(chosen, jnp.float32(0.0), shaped)  7.3 us
  transfers between devices with their start and end apart: 1, of which 1 were waited for; matrix products, arithmetic and copies ran while one was open for 4% of the time, Pallas kernels for 0%

commit v1 on v0

--- a/solution.py
+++ b/solution.py
@@ -1,6 +1,10 @@
+import functools
+
 import jax
 import jax.numpy as jnp
 from jax import lax
+from jax.experimental import pallas as pl
+from jax.experimental.pallas import tpu as pltpu
 from jax.sharding import PartitionSpec as P
 
 TILE = 128
@@ -94,7 +98,278 @@
     return (new_memory, master_new, first_new, second_new, step_blocks)
 
 
+def xor_bit(bit, flip):
+    return bit if flip == 0 else 1 - bit
+
+
+def pack_kernel(layers_smem, blocks_smem, grads_ref, memory_ref, master_ref, first_ref, second_ref,
+                out_ref, packed_ref, state_ref, member_ref):
+    layer, row = pl.program_id(0), pl.program_id(1)
+    tile_count = pl.num_programs(1)
+    count = layers_smem.shape[0]
+    layers = member_ref.shape[0]
+    pieces = state_ref.shape[1] // count
+
+    @pl.when((layer == 0) & (row == 0))
+    def _():
+        for k in range(count):
+            column = layers_smem[k] * (tile_count * tile_count) + blocks_smem[k]
+            for s, ref in enumerate((master_ref, first_ref, second_ref)):
+                line = ref[pl.ds(column, 1), :]
+                for j in range(pieces):
+                    state_ref[s, j * count + k:j * count + k + 1, :] = line[:, j * TILE:(j + 1) * TILE]
+            for l in range(layers):
+                flag = jnp.where(layers_smem[k] == l, jnp.float32(1.0), jnp.float32(0.0))
+                for j in range(pieces):
+                    member_ref[l, j * count + k:j * count + k + 1, :] = jnp.full((1, TILE), flag, jnp.float32)
+
+    memory = memory_ref[0].astype(jnp.float32)
+    total = grads_ref[0].astype(jnp.float32) + memory
+    out_ref[0] = ((1.0 - filter_rate) * memory + filter_rate * total).astype(out_ref.dtype)
+    for k in range(count):
+        block = blocks_smem[k]
+
+        @pl.when((layers_smem[k] == layer) & (lax.div(block, tile_count) == row))
+        def _():
+            lanes = pl.ds(pl.multiple_of(lax.rem(block, tile_count) * TILE, TILE), TILE)
+            kept = memory_ref[0, :, lanes].astype(jnp.float32)
+            packed_ref[pl.ds(k, TILE, stride=count), :] = grads_ref[0, :, lanes].astype(jnp.float32) + kept
+            out_ref[0, :, lanes] = ((1.0 - filter_rate) * kept).astype(out_ref.dtype)
+
+
+def exchange_kernel(n, packed_ref, state_ref, member_ref, rows_ref, step_ref,
+                    recv1, send2, recv2, send3, recv3, stat_own, stat_in, stat_mid, stat_far,
+                    s1, r1, s2, r2, s3, r3, s4, r4, s5, r5, sz, sp, sc, rg):
+    depth = n // 8
+    layers = member_ref.shape[0]
+    count = step_ref.shape[0]
+    entries = step_ref.shape[1] // n
+    pieces = entries // TILE
+    me = lax.axis_index("dp")
+    core = lax.rem(me, 2)
+    x = lax.rem(lax.div(me, 2), 2)
+    y = lax.rem(lax.div(me, 4), 2)
+    z = lax.div(me, 8)
+
+    def device(dz, dq, dc, back=False):
+        far = lax.rem(z + (depth - dz if back else dz), depth) if dz else z
+        return far * 8 + xor_bit(y, dq // 2) * 4 + xor_bit(x, dq % 2) * 2 + xor_bit(core, dc)
+
+    def plane(dq):
+        return xor_bit(y, dq // 2) * 2 + xor_bit(x, dq % 2)
+
+    def copy(src, dst, send, recv, peer):
+        return pltpu.make_async_remote_copy(
+            src_ref=src, dst_ref=dst, send_sem=send, recv_sem=recv,
+            device_id=(peer,), device_id_type=pl.DeviceIdType.MESH)
+
+    barrier = pltpu.get_barrier_semaphore()
+    peers = [device(0, i // 2, i % 2) for i in range(1, 8)] + [device(dz, 0, 0) for dz in range(1, depth)]
+    for peer in peers:
+        pl.semaphore_signal(barrier, inc=1, device_id=(peer,), device_id_type=pl.DeviceIdType.MESH)
+    pl.semaphore_wait(barrier, len(peers))
+
+    order = (3, 1, 2, 0)
+    first_hop = {}
+    for dq in order:
+        first_hop[dq] = copy(packed_ref.at[:, plane(dq), 1 - core], recv1.at[dq], s1.at[dq], r1.at[dq], device(0, 0, 1))
+        first_hop[dq].start()
+    second_hop = []
+    for dq in order[:3]:
+        first_hop[dq].wait_recv()
+        send2[dq - 1] = packed_ref[:, plane(dq), core] + recv1[dq]
+        hop = copy(send2.at[dq - 1], recv2.at[dq - 1], s2.at[dq - 1], r2.at[dq - 1], device(0, dq, 0))
+        hop.start()
+        second_hop.append(hop)
+    first_hop[0].wait_recv()
+    for hop in second_hop:
+        hop.wait_recv()
+    here = plane(0)
+
+    def plane_sum(at):
+        return (packed_ref[at, here, core] + recv1[0, at]) + ((recv2[0, at] + recv2[1, at]) + recv2[2, at])
+
+    third_hop = []
+    for dz in range(1, depth):
+        send3[dz - 1] = plane_sum(lax.rem(z + dz, depth))
+        hop = copy(send3.at[dz - 1], recv3.at[dz - 1], s3.at[dz - 1], r3.at[dz - 1], device(dz, 0, 0))
+        hop.start()
+        third_hop.append(hop)
+    summed = plane_sum(z)
+    for dz in range(1, depth):
+        third_hop[dz - 1].wait_recv()
+        summed = summed + recv3[dz - 1]
+
+    weights = state_ref[0]
+    first_sel = beta_one * state_ref[1] + (1.0 - beta_one) * summed
+    second_sel = beta_two * state_ref[2] + (1.0 - beta_two) * summed * summed
+    update = first_sel / (jnp.sqrt(second_sel) + adam_eps) + weight_decay * weights
+    rows_ref[1] = first_sel
+    rows_ref[2] = second_sel
+    stat_own[...] = jnp.zeros_like(stat_own)
+    for l in range(layers):
+        member = member_ref[l]
+        stat_own[l:l + 1, :] = jnp.sum(member * (weights * weights), axis=0, keepdims=True)
+        stat_own[layers + l:layers + l + 1, :] = jnp.sum(member * (update * update), axis=0, keepdims=True)
+    near = []
+    for i in range(1, 8):
+        hop = copy(stat_own, stat_in.at[i - 1], s4.at[i - 1], r4.at[i - 1], device(0, i // 2, i % 2))
+        hop.start()
+        near.append(hop)
+    total = stat_own[...]
+    for i in range(1, 8):
+        near[i - 1].wait_recv()
+        total = total + stat_in[i - 1]
+    stat_mid[...] = total
+    away = []
+    for dz in range(1, depth):
+        hop = copy(stat_mid, stat_far.at[dz - 1], s5.at[dz - 1], r5.at[dz - 1], device(dz, 0, 0))
+        hop.start()
+        away.append(hop)
+    for dz in range(1, depth):
+        away[dz - 1].wait_recv()
+        total = total + stat_far[dz - 1]
+    sums = jnp.sum(total, axis=1, keepdims=True)
+    factor = jnp.zeros_like(update)
+    for l in range(layers):
+        ratio = jnp.sqrt(sums[l:l + 1] / (sums[layers + l:layers + l + 1] + norm_eps))
+        factor = factor + member_ref[l] * ratio
+    scaled = factor * update
+    for j in range(pieces):
+        lanes = pl.ds(pl.multiple_of(me * entries + j * TILE, TILE), TILE)
+        step_ref[:, lanes] = scaled[j * count:(j + 1) * count].astype(step_ref.dtype)
+
+    def chunk(dz, dq, dc):
+        return step_ref.at[:, pl.ds(pl.multiple_of(device(dz, dq, dc, back=True) * entries, TILE), entries)]
+
+    started = list(near) + list(away) + second_hop + third_hop + list(first_hop.values())
+
+    def forward(dz, dq, dc, to_z, to_q, to_c, send, there):
+        block = chunk(dz, dq, dc)
+        hop = copy(block, block, send, rg.at[there], device(to_z, to_q, to_c))
+        hop.start()
+        started.append(hop)
+
+    def arrived(dz, dq, dc):
+        block = chunk(dz, dq, dc)
+        at = (dz * 4 + dq) * 2 + dc
+        copy(block, block, sz.at[0], rg.at[at], device(0, 0, 1)).wait_recv()
+
+    def spread(dz):
+        for dq in order[:3]:
+            forward(dz, 0, 0, 0, dq, 0, sp.at[dz * 3 + dq - 1], (dz * 4 + dq) * 2)
+
+    def hand_over(dz, dq):
+        forward(dz, dq, 0, 0, 0, 1, sc.at[dz * 4 + dq], (dz * 4 + dq) * 2 + 1)
+
+    for dz in range(1, depth):
+        forward(0, 0, 0, dz, 0, 0, sz.at[dz - 1], dz * 8)
+    spread(0)
+    hand_over(0, 0)
+    rows_ref[0] = weights - learn_rate * scaled
+    reach = sorted(range(1, depth), key=lambda dz: min(dz, depth - dz))
+    for at, dz in enumerate(reach):
+        arrived(dz, 0, 0)
+        spread(dz)
+        hand_over(dz, 0)
+    for dz in [0] + reach:
+        for dq in (1, 2, 3):
+            arrived(dz, dq, 0)
+            hand_over(dz, dq)
+    for dz in range(depth):
+        for dq in range(4):
+            arrived(dz, dq, 1)
+    for hop in started:
+        hop.wait_send()
+
+
+def state_kernel(layers_smem, blocks_smem, rows_ref, master_ref, first_ref, second_ref,
+                 master_out, first_out, second_out, *, layer_rows):
+    count = layers_smem.shape[0]
+    pieces = rows_ref.shape[1] // count
+    outs = ((master_ref, master_out), (first_ref, first_out), (second_ref, second_out))
+    for old, new in outs:
+        new[...] = old[...]
+    for k in range(count):
+        column = layers_smem[k] * layer_rows + blocks_smem[k]
+        base = pl.ds(pl.multiple_of(lax.div(column, 8) * 8, 8), 8)
+        hit = lax.broadcasted_iota(jnp.int32, (8, TILE), 0) == lax.rem(column, 8)
+        for s, (_, new) in enumerate(outs):
+            for j in range(pieces):
+                lanes = slice(j * TILE, (j + 1) * TILE)
+                line = rows_ref[s, j * count + k:j * count + k + 1, :]
+                new[base, lanes] = jnp.where(hit, line, new[base, lanes])
+
+
+def on_device_kernels(n, grads, memory, block_ids, layer_ids, master, first_moment, second_moment):
+    layers, width, _ = grads.shape
+    tile_count = width // TILE
+    count = block_ids.shape[0]
+    entries = master.shape[1]
+    lines = entries // TILE * count
+    depth = n // 8
+    f32 = jnp.float32
+    slab = pl.BlockSpec((1, TILE, width), lambda l, r, a, b: (l, r, 0))
+    whole = lambda shape: pl.BlockSpec(shape, lambda l, r, a, b: (0,) * len(shape))
+    new_memory, packed, state, member = pl.pallas_call(
+        pack_kernel,
+        grid_spec=pltpu.PrefetchScalarGridSpec(
+            num_scalar_prefetch=2, grid=(layers, tile_count),
+            in_specs=[slab, slab] + [whole(master.shape)] * 3,
+            out_specs=[slab, whole((n * lines, TILE)), whole((3, lines, TILE)), whole((layers, lines, TILE))]),
+        out_shape=[
+            jax.ShapeDtypeStruct(memory.shape, jnp.bfloat16),
+            jax.ShapeDtypeStruct((n * lines, TILE), f32),
+            jax.ShapeDtypeStruct((3, lines, TILE), f32),
+            jax.ShapeDtypeStruct((layers, lines, TILE), f32)],
+        name="pack",
+    )(layer_ids, block_ids, grads, memory, master, first_moment, second_moment)
+    vmem = pl.BlockSpec(memory_space=pltpu.VMEM)
+    stat_rows = -(-2 * layers // 8) * 8
+    dma = pltpu.SemaphoreType.DMA
+    rows, step_blocks = pl.pallas_call(
+        functools.partial(exchange_kernel, n),
+        out_shape=[jax.ShapeDtypeStruct((3, lines, TILE), f32),
+                   jax.ShapeDtypeStruct((count, n * entries), jnp.bfloat16)],
+        in_specs=[vmem] * 3,
+        out_specs=[vmem] * 2,
+        scratch_shapes=[
+            pltpu.VMEM((4, depth, lines, TILE), f32),
+            pltpu.VMEM((3, depth, lines, TILE), f32),
+            pltpu.VMEM((3, depth, lines, TILE), f32),
+            pltpu.VMEM((depth - 1, lines, TILE), f32),
+            pltpu.VMEM((depth - 1, lines, TILE), f32),
+            pltpu.VMEM((stat_rows, TILE), f32),
+            pltpu.VMEM((7, stat_rows, TILE), f32),
+            pltpu.VMEM((stat_rows, TILE), f32),
+            pltpu.VMEM((depth - 1, stat_rows, TILE), f32),
+            dma((4,)), dma((4,)), dma((3,)), dma((3,)), dma((depth - 1,)), dma((depth - 1,)),
+            dma((7,)), dma((7,)), dma((depth - 1,)), dma((depth - 1,)),
+            dma((depth - 1,)), dma((depth * 3,)), dma((depth * 4,)), dma((n,))],
+        compiler_params=pltpu.CompilerParams(collective_id=0, has_side_effects=True),
+        name="exchange",
+    )(packed.reshape(depth, 4, 2, lines, TILE), state, member)
+    smem = pl.BlockSpec(memory_space=pltpu.SMEM)
+    like = jax.ShapeDtypeStruct(master.shape, f32)
+    master_new, first_new, second_new = pl.pallas_call(
+        functools.partial(state_kernel, layer_rows=tile_count * tile_count),
+        out_shape=[like] * 3,
+        in_specs=[smem, smem] + [vmem] * 4,
+        out_specs=[vmem] * 3,
+        name="state",
+    )(layer_ids, block_ids, rows, master, first_moment, second_moment)
+    return (new_memory, master_new, first_new, second_new, step_blocks)
+
+
 def solution(mesh):
+    n = mesh.shape["dp"]
+
+    def body(*args):
+        entries, count = args[4].shape[1], args[2].shape[0]
+        if n % 8 == 0 and n > 8 and entries % TILE == 0 and count % 16 == 0:
+            return on_device_kernels(n, *args)
+        return on_device(*args)
+
     in_specs = (
         P("dp", None, None),
         P("dp", None, None),
@@ -106,5 +381,5 @@
     )
     out_specs = (P("dp", None, None), P(None, "dp"), P(None, "dp"), P(None, "dp"), P())
     return jax.shard_map(
-        on_device, mesh=mesh, in_specs=in_specs, out_specs=out_specs, check_vma=False
-    )
+        body, mesh=mesh, in_specs=in_specs, out_specs=out_specs, check_vma=False
+    )

time: 358 us -> 56.8 us (0.16)
  local copies, waits for them, and re-layouts: 127 us -> 1.87 us
  waiting for transfers between devices: 124 us -> 0 us
  blocking collectives: 78.1 us -> 0 us
  Pallas kernels: 0 us -> 53.8 us
  between operations: 14.2 us -> 0.64 us
  other arithmetic: 11.5 us -> 0 us
    reduce_scatter x1 -> x0, waiting for transfers between devices: 124 us -> none  [on_device(): summed = lax.psum_scatter(packed, 'dp', scatter_dimension=1, tiled=True)]
    gather x99 -> x0, local copies, waits for them, and re-layouts: 114 us -> none
    pallas_call x0 -> x3, Pallas kernels: none -> 53.8 us  [the longest x1 36.9 us: on_device_kernels(): pl.pallas_call(functools.partial(exchange_kernel, n), out_shape=[jax.Shap...]
    all_gather x1 -> x0, blocking collectives: 41.3 us -> none  [on_device(): lax.all_gather(scaled.astype(jnp.bfloat16), 'dp', axis=1, tiled=True)]
    psum x1 -> x0, blocking collectives: 36.9 us -> none  [on_device(): lax.psum((layer_squares(member, weights_sel), layer_squares(member, updat...]
    broadcast_in_dim x3 -> x0, local copies, waits for them, and re-layouts: 7.3 us -> none  [filter_memory(): jnp.where(chosen, jnp.float32(0.0), shaped)]
    convert_element_type x2 -> x0, other arithmetic: 6.3 us -> none  [the longest x1 6.23 us: filter_memory(): return mixed.astype(jnp.bfloat16)]
    unnamed x17 -> x1, local copies, waits for them, and re-layouts: 5.55 us -> 1.87 us
  transfers between devices with their start and end apart: 1 -> 0, of which waited for: 1 -> 0; matrix products, arithmetic and copies ran while one was open for 4% -> 0% of each run, Pallas kernels for 0% -> 0%
where the time goes in v1:
time: 56.8 us; the launch traced here: 56.3 us
  Pallas kernels  53.8 us (95%)
  local copies, waits for them, and re-layouts  1.87 us (3%)
  between operations  0.64 us (1%)
    pallas_call x1, Pallas kernels, on_device_kernels(): pl.pallas_call(functools.partial(exchange_kernel, n), out_shape=[jax.Shap...  36.9 us
    pallas_call x1, Pallas kernels, on_device_kernels(): pl.pallas_call(pack_kernel, grid_spec=pltpu.PrefetchScalarGridSpec(num_sc...  14.8 us
    pallas_call x1, Pallas kernels, on_device_kernels(): pl.pallas_call(functools.partial(state_kernel, layer_rows=tile_count * ti...  2.15 us
    unnamed x1, local copies, waits for them, and re-layouts  1.87 us

profile of v1, /device:TPU:0, one launch (start us, length us, event | category | flops | bytes accessed | tf_op | source)
XLA Modules:
  0.0 56.3 jit_solution(5935889498262302762)
XLA Ops:
  0.6 14.8 %pack.1 = (bf16[2,1024,1024]{2,1,0:T(8,128)(2,1)}, f32[2048,128]{1,0:T(8,128)}, f32[3,64,128]{2,1,0:T(8,128)}, f32[2,64,128]{2,1,0:T(8,128)}) custom-call(s32[16]{0:T(128)} %layers_smem.3, s32[16]{0:T(128)} %blocks_smem.3, bf16[2,1024,1024]{2,1,0:T(8,128)(2,1)} %grads_ref.1, bf16[2,1024,1024]{2,1,0:T(8,128)(2,1)} %memory_ref.1, f32[128,512]{1,0:T(8,128)} %master_ref.3, ...), custom_call_target="tpu_custom_call" | custom-call | tf_op jit(solution)/shard_map/pack/pallas_call | solution.py:314
  15.4 36.9 %exchange.1 = (f32[3,64,128]{2,1,0:T(8,128)}, bf16[16,16384]{1,0:T(8,128)(2,1)}) custom-call(f32[4,4,2,64,128]{4,3,2,1,0:T(8,128)} %bitcast.1, f32[3,64,128]{2,1,0:T(8,128)} %get-tuple-element.16.state_ref, f32[2,64,128]{2,1,0:T(8,128)} %get-tuple-element.17.member_ref), custom_call_target="tpu_custom_call" | custom-call | tf_op jit(solution)/shard_map/exchange/pallas_call | solution.py:330
  52.3 2.1 %state.1 = (f32[128,512]{1,0:T(8,128)}, f32[128,512]{1,0:T(8,128)}, f32[128,512]{1,0:T(8,128)}) custom-call(s32[16]{0:T(128)} %layers_smem.3, s32[16]{0:T(128)} %blocks_smem.3, f32[3,64,128]{2,1,0:T(8,128)} %get-tuple-element.18.rows_ref, f32[128,512]{1,0:T(8,128)} %master_ref.3, f32[128,512]{1,0:T(8,128)} %first_ref.3, f32[128,512]{1,0:T(8,128)} %second_ref.3), custom_call_target="tpu_custom_call" | custom-call | tf_op jit(solution)/shard_map/state/pallas_call | solution.py:354
  54.4 1.9 %copy.13 = bf16[16,16384]{1,0:T(8,128)(2,1)} copy(bf16[16,16384]{1,0:T(8,128)(2,1)} %get-tuple-element.32) | data formatting | bytes 1048576

commit v2 on v1

--- a/solution.py
+++ b/solution.py
@@ -102,44 +102,64 @@
     return bit if flip == 0 else 1 - bit
 
 
-def pack_kernel(layers_smem, blocks_smem, grads_ref, memory_ref, master_ref, first_ref, second_ref,
-                out_ref, packed_ref, state_ref, member_ref):
-    layer, row = pl.program_id(0), pl.program_id(1)
-    tile_count = pl.num_programs(1)
+def pack_kernel(layers_smem, blocks_smem, grads_hbm, memory_hbm, master_ref, first_ref, second_ref,
+                out_hbm, packed_ref, state_ref, member_ref,
+                grads_ref, memory_ref, out_ref, grads_sem, memory_sem, out_sem):
     count = layers_smem.shape[0]
     layers = member_ref.shape[0]
     pieces = state_ref.shape[1] // count
-
-    @pl.when((layer == 0) & (row == 0))
-    def _():
+    slabs = grads_ref.shape[0]
+    tile_count = slabs // layers
+
+    def moves(i):
+        layer, rows = lax.div(i, tile_count), pl.ds(lax.rem(i, tile_count) * TILE, TILE)
+        return (pltpu.make_async_copy(grads_hbm.at[layer, rows], grads_ref.at[i], grads_sem.at[i]),
+                pltpu.make_async_copy(memory_hbm.at[layer, rows], memory_ref.at[i], memory_sem.at[i]),
+                pltpu.make_async_copy(out_ref.at[i], out_hbm.at[layer, rows], out_sem.at[i]))
+
+    @pl.loop(0, slabs)
+    def _(i):
+        moves(i)[0].start()
+        moves(i)[1].start()
+
+    for k in range(count):
+        column = layers_smem[k] * (tile_count * tile_count) + blocks_smem[k]
+        for s, ref in enumerate((master_ref, first_ref, second_ref)):
+            line = ref[pl.ds(column, 1), :]
+            for j in range(pieces):
+                state_ref[s, j * count + k:j * count + k + 1, :] = line[:, j * TILE:(j + 1) * TILE]
+        for l in range(layers):
+            flag = jnp.where(layers_smem[k] == l, jnp.float32(1.0), jnp.float32(0.0))
+            for j in range(pieces):
+                member_ref[l, j * count + k:j * count + k + 1, :] = jnp.full((1, TILE), flag, jnp.float32)
+
+    @pl.loop(0, slabs)
+    def _(i):
+        moves(i)[0].wait()
+        moves(i)[1].wait()
+        memory = memory_ref[i].astype(jnp.float32)
+        total = grads_ref[i].astype(jnp.float32) + memory
+        out_ref[i] = ((1.0 - filter_rate) * memory + filter_rate * total).astype(out_ref.dtype)
         for k in range(count):
-            column = layers_smem[k] * (tile_count * tile_count) + blocks_smem[k]
-            for s, ref in enumerate((master_ref, first_ref, second_ref)):
-                line = ref[pl.ds(column, 1), :]
-                for j in range(pieces):
-                    state_ref[s, j * count + k:j * count + k + 1, :] = line[:, j * TILE:(j + 1) * TILE]
-            for l in range(layers):
-                flag = jnp.where(layers_smem[k] == l, jnp.float32(1.0), jnp.float32(0.0))
-                for j in range(pieces):
-                    member_ref[l, j * count + k:j * count + k + 1, :] = jnp.full((1, TILE), flag, jnp.float32)
-
-    memory = memory_ref[0].astype(jnp.float32)
-    total = grads_ref[0].astype(jnp.float32) + memory
-    out_ref[0] = ((1.0 - filter_rate) * memory + filter_rate * total).astype(out_ref.dtype)
-    for k in range(count):
-        block = blocks_smem[k]
-
-        @pl.when((layers_smem[k] == layer) & (lax.div(block, tile_count) == row))
-        def _():
-            lanes = pl.ds(pl.multiple_of(lax.rem(block, tile_count) * TILE, TILE), TILE)
-            kept = memory_ref[0, :, lanes].astype(jnp.float32)
-            packed_ref[pl.ds(k, TILE, stride=count), :] = grads_ref[0, :, lanes].astype(jnp.float32) + kept
-            out_ref[0, :, lanes] = ((1.0 - filter_rate) * kept).astype(out_ref.dtype)
+            block = blocks_smem[k]
+
+            @pl.when(layers_smem[k] * tile_count + lax.div(block, tile_count) == i)
+            def _():
+                lanes = pl.ds(pl.multiple_of(lax.rem(block, tile_count) * TILE, TILE), TILE)
+                kept = memory_ref[i, :, lanes].astype(jnp.float32)
+                packed_ref[pl.ds(k, TILE, stride=count), :] = grads_ref[i, :, lanes].astype(jnp.float32) + kept
+                out_ref[i, :, lanes] = ((1.0 - filter_rate) * kept).astype(out_ref.dtype)
+
+        moves(i)[2].start()
+
+    @pl.loop(0, slabs)
+    def _(i):
+        moves(i)[2].wait()
 
 
 def exchange_kernel(n, packed_ref, state_ref, member_ref, rows_ref, step_ref,
-                    recv1, send2, recv2, send3, recv3, stat_own, stat_in, stat_mid, stat_far,
-                    s1, r1, s2, r2, s3, r3, s4, r4, s5, r5, sz, sp, sc, rg):
+                    mine, recv1, send2, recv2, send3, recv3, stat_own, stat_in, stat_mid, stat_far,
+                    s0, s1, r1, s2, r2, s3, r3, s4, r4, s5, r5, sz, sp, sc, rg):
     depth = n // 8
     layers = member_ref.shape[0]
     count = step_ref.shape[0]
@@ -167,50 +187,56 @@
     peers = [device(0, i // 2, i % 2) for i in range(1, 8)] + [device(dz, 0, 0) for dz in range(1, depth)]
     for peer in peers:
         pl.semaphore_signal(barrier, inc=1, device_id=(peer,), device_id_type=pl.DeviceIdType.MESH)
+    own_half = pltpu.make_async_copy(packed_ref.at[:, :, core], mine, s0.at[0])
+    own_half.start()
+    weights = state_ref[0]
+    stat_own[...] = jnp.zeros_like(stat_own)
+    for l in range(layers):
+        stat_own[l:l + 1, :] = jnp.sum(member_ref[l] * (weights * weights), axis=0, keepdims=True)
     pl.semaphore_wait(barrier, len(peers))
 
     order = (3, 1, 2, 0)
-    first_hop = {}
-    for dq in order:
-        first_hop[dq] = copy(packed_ref.at[:, plane(dq), 1 - core], recv1.at[dq], s1.at[dq], r1.at[dq], device(0, 0, 1))
-        first_hop[dq].start()
-    second_hop = []
-    for dq in order[:3]:
-        first_hop[dq].wait_recv()
-        send2[dq - 1] = packed_ref[:, plane(dq), core] + recv1[dq]
-        hop = copy(send2.at[dq - 1], recv2.at[dq - 1], s2.at[dq - 1], r2.at[dq - 1], device(0, dq, 0))
-        hop.start()
-        second_hop.append(hop)
-    first_hop[0].wait_recv()
-    for hop in second_hop:
-        hop.wait_recv()
+    reach = sorted(range(1, depth), key=lambda dz: min(dz, depth - dz))
+    targets = [(dz, lax.rem(z + dz, depth)) for dz in reach[::-1]] + [(0, z)]
+    first_hop, second_hop, third_hop = {}, {}, {}
+    for dz, at in targets:
+        for dq in order:
+            slot = dz * 4 + dq
+            first_hop[slot] = copy(packed_ref.at[at, plane(dq), 1 - core], recv1.at[slot],
+                                   s1.at[slot], r1.at[slot], device(0, 0, 1))
+            first_hop[slot].start()
+    own_half.wait()
+    for dz, at in targets:
+        for dq in order[:3]:
+            slot, place = dz * 4 + dq, dz * 3 + dq - 1
+            first_hop[slot].wait_recv()
+            send2[place] = mine[at, plane(dq)] + recv1[slot]
+            second_hop[place] = copy(send2.at[place], recv2.at[place], s2.at[place], r2.at[place], device(0, dq, 0))
+            second_hop[place].start()
     here = plane(0)
-
-    def plane_sum(at):
-        return (packed_ref[at, here, core] + recv1[0, at]) + ((recv2[0, at] + recv2[1, at]) + recv2[2, at])
-
-    third_hop = []
+    summed = None
+    for dz, at in targets:
+        first_hop[dz * 4].wait_recv()
+        for dq in range(3):
+            second_hop[dz * 3 + dq].wait_recv()
+        part = (mine[at, here] + recv1[dz * 4]) + ((recv2[dz * 3] + recv2[dz * 3 + 1]) + recv2[dz * 3 + 2])
+        if dz == 0:
+            summed = part
+        else:
+            send3[dz - 1] = part
+            third_hop[dz] = copy(send3.at[dz - 1], recv3.at[dz - 1], s3.at[dz - 1], r3.at[dz - 1], device(dz, 0, 0))
+            third_hop[dz].start()
     for dz in range(1, depth):
-        send3[dz - 1] = plane_sum(lax.rem(z + dz, depth))
-        hop = copy(send3.at[dz - 1], recv3.at[dz - 1], s3.at[dz - 1], r3.at[dz - 1], device(dz, 0, 0))
-        hop.start()
-        third_hop.append(hop)
-    summed = plane_sum(z)
-    for dz in range(1, depth):
-        third_hop[dz - 1].wait_recv()
+        third_hop[dz].wait_recv()
         summed = summed + recv3[dz - 1]
 
-    weights = state_ref[0]
     first_sel = beta_one * state_ref[1] + (1.0 - beta_one) * summed
     second_sel = beta_two * state_ref[2] + (1.0 - beta_two) * summed * summed
     update = first_sel / (jnp.sqrt(second_sel) + adam_eps) + weight_decay * weights
     rows_ref[1] = first_sel
     rows_ref[2] = second_sel
-    stat_own[...] = jnp.zeros_like(stat_own)
     for l in range(layers):
-        member = member_ref[l]
-        stat_own[l:l + 1, :] = jnp.sum(member * (weights * weights), axis=0, keepdims=True)
-        stat_own[layers + l:layers + l + 1, :] = jnp.sum(member * (update * update), axis=0, keepdims=True)
+        stat_own[layers + l:layers + l + 1, :] = jnp.sum(member_ref[l] * (update * update), axis=0, keepdims=True)
     near = []
     for i in range(1, 8):
         hop = copy(stat_own, stat_in.at[i - 1], s4.at[i - 1], r4.at[i - 1], device(0, i // 2, i % 2))
@@ -242,7 +268,7 @@
     def chunk(dz, dq, dc):
         return step_ref.at[:, pl.ds(pl.multiple_of(device(dz, dq, dc, back=True) * entries, TILE), entries)]
 
-    started = list(near) + list(away) + second_hop + third_hop + list(first_hop.values())
+    started = near + away + [hop for hops in (first_hop, second_hop, third_hop) for hop in hops.values()]
 
     def forward(dz, dq, dc, to_z, to_q, to_c, send, there):
         block = chunk(dz, dq, dc)
@@ -267,8 +293,7 @@
     spread(0)
     hand_over(0, 0)
     rows_ref[0] = weights - learn_rate * scaled
-    reach = sorted(range(1, depth), key=lambda dz: min(dz, depth - dz))
-    for at, dz in enumerate(reach):
+    for dz in reach:
         arrived(dz, 0, 0)
         spread(dz)
         hand_over(dz, 0)
@@ -283,11 +308,12 @@
         hop.wait_send()
 
 
-def state_kernel(layers_smem, blocks_smem, rows_ref, master_ref, first_ref, second_ref,
-                 master_out, first_out, second_out, *, layer_rows):
+def state_kernel(layers_smem, blocks_smem, rows_ref, step_ref, master_ref, first_ref, second_ref,
+                 master_out, first_out, second_out, step_out, *, layer_rows):
     count = layers_smem.shape[0]
     pieces = rows_ref.shape[1] // count
     outs = ((master_ref, master_out), (first_ref, first_out), (second_ref, second_out))
+    step_out[...] = step_ref[...]
     for old, new in outs:
         new[...] = old[...]
     for k in range(count):
@@ -309,55 +335,53 @@
     lines = entries // TILE * count
     depth = n // 8
     f32 = jnp.float32
-    slab = pl.BlockSpec((1, TILE, width), lambda l, r, a, b: (l, r, 0))
-    whole = lambda shape: pl.BlockSpec(shape, lambda l, r, a, b: (0,) * len(shape))
+    vmem, smem, hbm = (pl.BlockSpec(memory_space=m) for m in (pltpu.VMEM, pltpu.SMEM, pl.ANY))
+    slabs = layers * tile_count
+    dma = pltpu.SemaphoreType.DMA
     new_memory, packed, state, member = pl.pallas_call(
         pack_kernel,
-        grid_spec=pltpu.PrefetchScalarGridSpec(
-            num_scalar_prefetch=2, grid=(layers, tile_count),
-            in_specs=[slab, slab] + [whole(master.shape)] * 3,
-            out_specs=[slab, whole((n * lines, TILE)), whole((3, lines, TILE)), whole((layers, lines, TILE))]),
+        in_specs=[smem, smem, hbm, hbm] + [vmem] * 3,
+        out_specs=[hbm] + [vmem] * 3,
         out_shape=[
             jax.ShapeDtypeStruct(memory.shape, jnp.bfloat16),
             jax.ShapeDtypeStruct((n * lines, TILE), f32),
             jax.ShapeDtypeStruct((3, lines, TILE), f32),
             jax.ShapeDtypeStruct((layers, lines, TILE), f32)],
+        scratch_shapes=[pltpu.VMEM((slabs, TILE, width), jnp.bfloat16)] * 3 + [dma((slabs,))] * 3,
         name="pack",
     )(layer_ids, block_ids, grads, memory, master, first_moment, second_moment)
-    vmem = pl.BlockSpec(memory_space=pltpu.VMEM)
     stat_rows = -(-2 * layers // 8) * 8
-    dma = pltpu.SemaphoreType.DMA
-    rows, step_blocks = pl.pallas_call(
+    rows, gathered = pl.pallas_call(
         functools.partial(exchange_kernel, n),
         out_shape=[jax.ShapeDtypeStruct((3, lines, TILE), f32),
                    jax.ShapeDtypeStruct((count, n * entries), jnp.bfloat16)],
-        in_specs=[vmem] * 3,
+        in_specs=[hbm, vmem, vmem],
         out_specs=[vmem] * 2,
         scratch_shapes=[
-            pltpu.VMEM((4, depth, lines, TILE), f32),
-            pltpu.VMEM((3, depth, lines, TILE), f32),
-            pltpu.VMEM((3, depth, lines, TILE), f32),
+            pltpu.VMEM((depth, 4, lines, TILE), f32),
+            pltpu.VMEM((depth * 4, lines, TILE), f32),
+            pltpu.VMEM((depth * 3, lines, TILE), f32),
+            pltpu.VMEM((depth * 3, lines, TILE), f32),
             pltpu.VMEM((depth - 1, lines, TILE), f32),
             pltpu.VMEM((depth - 1, lines, TILE), f32),
             pltpu.VMEM((stat_rows, TILE), f32),
             pltpu.VMEM((7, stat_rows, TILE), f32),
             pltpu.VMEM((stat_rows, TILE), f32),
             pltpu.VMEM((depth - 1, stat_rows, TILE), f32),
-            dma((4,)), dma((4,)), dma((3,)), dma((3,)), dma((depth - 1,)), dma((depth - 1,)),
+            dma((1,)), dma((depth * 4,)), dma((depth * 4,)), dma((depth * 3,)), dma((depth * 3,)), dma((depth - 1,)), dma((depth - 1,)),
             dma((7,)), dma((7,)), dma((depth - 1,)), dma((depth - 1,)),
             dma((depth - 1,)), dma((depth * 3,)), dma((depth * 4,)), dma((n,))],
         compiler_params=pltpu.CompilerParams(collective_id=0, has_side_effects=True),
         name="exchange",
     )(packed.reshape(depth, 4, 2, lines, TILE), state, member)
-    smem = pl.BlockSpec(memory_space=pltpu.SMEM)
     like = jax.ShapeDtypeStruct(master.shape, f32)
-    master_new, first_new, second_new = pl.pallas_call(
+    master_new, first_new, second_new, step_blocks = pl.pallas_call(
         functools.partial(state_kernel, layer_rows=tile_count * tile_count),
-        out_shape=[like] * 3,
-        in_specs=[smem, smem] + [vmem] * 4,
-        out_specs=[vmem] * 3,
+        out_shape=[like] * 3 + [jax.ShapeDtypeStruct(gathered.shape, jnp.bfloat16)],
+        in_specs=[smem, smem] + [vmem] * 5,
+        out_specs=[vmem] * 4,
         name="state",
-    )(layer_ids, block_ids, rows, master, first_moment, second_moment)
+    )(layer_ids, block_ids, rows, gathered, master, first_moment, second_moment)
     return (new_memory, master_new, first_new, second_new, step_blocks)
 
 

time: 56.8 us -> 48.4 us (0.85)
  Pallas kernels: 53.8 us -> 47.6 us
  local copies, waits for them, and re-layouts: 1.87 us -> 0 us
    pallas_call x1, Pallas kernels: 14.8 us -> 9.68 us  [on_device_kernels(): pl.pallas_call(pack_kernel, in_specs=[smem, smem, hbm, hbm] + [vmem] * 3,...]
    unnamed x1 -> x0, local copies, waits for them, and re-layouts: 1.87 us -> none
    pallas_call x1, Pallas kernels: 36.9 us -> 35.4 us  [on_device_kernels(): pl.pallas_call(functools.partial(exchange_kernel, n), out_shape=[jax.Shap...]
where the time goes in v2:
time: 48.4 us; the launch traced here: 48.2 us
  Pallas kernels  47.6 us (98%)
  between operations  0.65 us (1%)
    pallas_call x1, Pallas kernels, on_device_kernels(): pl.pallas_call(functools.partial(exchange_kernel, n), out_shape=[jax.Shap...  35.4 us
    pallas_call x1, Pallas kernels, on_device_kernels(): pl.pallas_call(pack_kernel, in_specs=[smem, smem, hbm, hbm] + [vmem] * 3,...  9.68 us
    pallas_call x1, Pallas kernels, on_device_kernels(): pl.pallas_call(functools.partial(state_kernel, layer_rows=tile_count * ti...  2.47 us

profile of v2, /device:TPU:0, one launch (start us, length us, event | category | flops | bytes accessed | tf_op | source)
XLA Modules:
  0.0 48.2 jit_solution(3504258614961736717)
XLA Ops:
  0.6 9.7 %pack.1 = (bf16[2,1024,1024]{2,1,0:T(8,128)(2,1)}, f32[2048,128]{1,0:T(8,128)}, f32[3,64,128]{2,1,0:T(8,128)}, f32[2,64,128]{2,1,0:T(8,128)}) custom-call(s32[16]{0:T(128)} %layers_smem.3, s32[16]{0:T(128)} %blocks_smem.3, bf16[2,1024,1024]{2,1,0:T(8,128)(2,1)} %grads_hbm.1, bf16[2,1024,1024]{2,1,0:T(8,128)(2,1)} %memory_hbm.1, f32[128,512]{1,0:T(8,128)} %master_ref.3, ...), custom_call_target="tpu_custom_call" | custom-call | tf_op jit(solution)/shard_map/pack/pallas_call | solution.py:341
  10.3 35.4 %exchange.1 = (f32[3,64,128]{2,1,0:T(8,128)}, bf16[16,16384]{1,0:T(8,128)(2,1)}) custom-call(f32[4,4,2,64,128]{4,3,2,1,0:T(8,128)} %bitcast.1, f32[3,64,128]{2,1,0:T(8,128)} %get-tuple-element.17.state_ref, f32[2,64,128]{2,1,0:T(8,128)} %get-tuple-element.18.member_ref), custom_call_target="tpu_custom_call" | custom-call | tf_op jit(solution)/shard_map/exchange/pallas_call | solution.py:354
  45.7 2.5 %state.1 = (f32[128,512]{1,0:T(8,128)}, f32[128,512]{1,0:T(8,128)}, f32[128,512]{1,0:T(8,128)}, bf16[16,16384]{1,0:T(8,128)(2,1)}) custom-call(s32[16]{0:T(128)} %layers_smem.3, s32[16]{0:T(128)} %blocks_smem.3, f32[3,64,128]{2,1,0:T(8,128)} %get-tuple-element.19.rows_ref, bf16[16,16384]{1,0:T(8,128)(2,1)} %get-tuple-element.20.step_ref, ...), custom_call_target="tpu_custom_call" | custom-call | tf_op jit(solution)/shard_map/state/pallas_call | solution.py:378

commit v3 on v2

--- a/solution.py
+++ b/solution.py
@@ -102,9 +102,10 @@
     return bit if flip == 0 else 1 - bit
 
 
-def pack_kernel(layers_smem, blocks_smem, grads_hbm, memory_hbm, master_ref, first_ref, second_ref,
-                out_hbm, packed_ref, state_ref, member_ref,
-                grads_ref, memory_ref, out_ref, grads_sem, memory_sem, out_sem):
+def pack_kernel(layers_smem, blocks_smem, grads_hbm, memory_hbm, master_hbm, first_hbm, second_hbm,
+                out_hbm, packed_hbm, state_ref, member_ref,
+                grads_ref, memory_ref, out_ref, grad_tiles, memory_tiles, packed_ref, old_ref, rate_ref,
+                grads_sem, memory_sem, out_sem, tile_sem, old_sem, packed_sem):
     count = layers_smem.shape[0]
     layers = member_ref.shape[0]
     pieces = state_ref.shape[1] // count
@@ -112,54 +113,82 @@
     tile_count = slabs // layers
 
     def moves(i):
-        layer, rows = lax.div(i, tile_count), pl.ds(lax.rem(i, tile_count) * TILE, TILE)
-        return (pltpu.make_async_copy(grads_hbm.at[layer, rows], grads_ref.at[i], grads_sem.at[i]),
-                pltpu.make_async_copy(memory_hbm.at[layer, rows], memory_ref.at[i], memory_sem.at[i]),
-                pltpu.make_async_copy(out_ref.at[i], out_hbm.at[layer, rows], out_sem.at[i]))
+        layer, rows = lax.div(i, tile_count), pl.ds(pl.multiple_of(lax.rem(i, tile_count) * TILE, TILE), TILE)
+        return ((grads_hbm.at[layer, rows], grads_ref.at[i], grads_sem.at[i]),
+                (memory_hbm.at[layer, rows], memory_ref.at[i], memory_sem.at[i]),
+                (out_ref.at[i], out_hbm.at[layer, rows], out_sem.at[i]))
+
+    tiles = []
+    for k in range(count):
+        block = blocks_smem[k]
+        rows = pl.ds(pl.multiple_of(lax.div(block, tile_count) * TILE, TILE), TILE)
+        lanes = pl.ds(pl.multiple_of(lax.rem(block, tile_count) * TILE, TILE), TILE)
+        for s, (source, held) in enumerate(((grads_hbm, grad_tiles), (memory_hbm, memory_tiles))):
+            tiles.append(pltpu.make_async_copy(
+                source.at[layers_smem[k], rows, lanes], held.at[k], tile_sem.at[s * count + k]))
+            tiles[-1].start()
 
     @pl.loop(0, slabs)
     def _(i):
-        moves(i)[0].start()
-        moves(i)[1].start()
-
+        grads_in, memory_in, _ = moves(i)
+        pltpu.make_async_copy(*grads_in).start()
+        pltpu.make_async_copy(*memory_in).start()
+
+    olds = []
+    for s, source in enumerate((master_hbm, first_hbm, second_hbm)):
+        olds.append(pltpu.make_async_copy(source, old_ref.at[s], old_sem.at[s]))
+        olds[-1].start()
+
+    @pl.loop(0, slabs)
+    def _(i):
+        for t in range(tile_count):
+            rate_ref[i * tile_count + t] = jnp.float32(filter_rate)
+
+    for k in range(count):
+        rate_ref[layers_smem[k] * (tile_count * tile_count) + blocks_smem[k]] = jnp.float32(0.0)
+    for k in range(count):
+        tiles[2 * k].wait()
+        tiles[2 * k + 1].wait()
+        packed_ref[pl.ds(k, TILE, stride=count), :] = (
+            grad_tiles[k].astype(jnp.float32) + memory_tiles[k].astype(jnp.float32))
+    packed_out = pltpu.make_async_copy(packed_ref, packed_hbm, packed_sem.at[0])
+    packed_out.start()
+
+    @pl.loop(0, slabs)
+    def _(i):
+        grads_in, memory_in, out = moves(i)
+        pltpu.make_async_copy(*grads_in).wait()
+        pltpu.make_async_copy(*memory_in).wait()
+        for t in range(tile_count):
+            lanes = slice(t * TILE, (t + 1) * TILE)
+            memory = memory_ref[i, :, lanes].astype(jnp.float32)
+            total = grads_ref[i, :, lanes].astype(jnp.float32) + memory
+            mixed = (1.0 - filter_rate) * memory + rate_ref[i * tile_count + t] * total
+            out_ref[i, :, lanes] = mixed.astype(out_ref.dtype)
+        pltpu.make_async_copy(*out).start()
+
+    for old in olds:
+        old.wait()
     for k in range(count):
         column = layers_smem[k] * (tile_count * tile_count) + blocks_smem[k]
-        for s, ref in enumerate((master_ref, first_ref, second_ref)):
-            line = ref[pl.ds(column, 1), :]
+        for s in range(3):
+            line = old_ref[s, pl.ds(column, 1), :]
             for j in range(pieces):
                 state_ref[s, j * count + k:j * count + k + 1, :] = line[:, j * TILE:(j + 1) * TILE]
         for l in range(layers):
             flag = jnp.where(layers_smem[k] == l, jnp.float32(1.0), jnp.float32(0.0))
             for j in range(pieces):
                 member_ref[l, j * count + k:j * count + k + 1, :] = jnp.full((1, TILE), flag, jnp.float32)
+    packed_out.wait()
 
     @pl.loop(0, slabs)
     def _(i):
-        moves(i)[0].wait()
-        moves(i)[1].wait()
-        memory = memory_ref[i].astype(jnp.float32)
-        total = grads_ref[i].astype(jnp.float32) + memory
-        out_ref[i] = ((1.0 - filter_rate) * memory + filter_rate * total).astype(out_ref.dtype)
-        for k in range(count):
-            block = blocks_smem[k]
-
-            @pl.when(layers_smem[k] * tile_count + lax.div(block, tile_count) == i)
-            def _():
-                lanes = pl.ds(pl.multiple_of(lax.rem(block, tile_count) * TILE, TILE), TILE)
-                kept = memory_ref[i, :, lanes].astype(jnp.float32)
-                packed_ref[pl.ds(k, TILE, stride=count), :] = grads_ref[i, :, lanes].astype(jnp.float32) + kept
-                out_ref[i, :, lanes] = ((1.0 - filter_rate) * kept).astype(out_ref.dtype)
-
-        moves(i)[2].start()
-
-    @pl.loop(0, slabs)
-    def _(i):
-        moves(i)[2].wait()
+        pltpu.make_async_copy(*moves(i)[2]).wait()
 
 
 def exchange_kernel(n, packed_ref, state_ref, member_ref, rows_ref, step_ref,
-                    mine, recv1, send2, recv2, send3, recv3, stat_own, stat_in, stat_mid, stat_far,
-                    s0, s1, r1, s2, r2, s3, r3, s4, r4, s5, r5, sz, sp, sc, rg):
+                    mine, recv1, send2, recv2, send3, recv3, stat_own, stat_in, stat_mid, stat_far, update_own, update_far,
+                    s0, s1, r1, s2, r2, s3, r3, s4, r4, s5, r5, sz, rz, sp, sc, rg):
     depth = n // 8
     layers = member_ref.shape[0]
     count = step_ref.shape[0]
@@ -237,38 +266,51 @@
     rows_ref[2] = second_sel
     for l in range(layers):
         stat_own[layers + l:layers + l + 1, :] = jnp.sum(member_ref[l] * (update * update), axis=0, keepdims=True)
-    near = []
+    def spot(dq, dc):
+        return plane(dq) * 2 + xor_bit(core, dc)
+
+    near, away, ahead = [], [], {}
     for i in range(1, 8):
-        hop = copy(stat_own, stat_in.at[i - 1], s4.at[i - 1], r4.at[i - 1], device(0, i // 2, i % 2))
-        hop.start()
-        near.append(hop)
-    total = stat_own[...]
+        near.append(copy(stat_own, stat_in.at[spot(0, 0)], s4.at[i - 1], r4.at[i - 1], device(0, i // 2, i % 2)))
+        near[-1].start()
+    update_own[...] = update
+    for dz in range(1, depth):
+        ahead[dz] = copy(update_own, update_far.at[dz - 1], sz.at[dz - 1], rz.at[dz - 1], device(dz, 0, 0))
+        ahead[dz].start()
+    stat_in[spot(0, 0)] = stat_own[...]
     for i in range(1, 8):
-        near[i - 1].wait_recv()
-        total = total + stat_in[i - 1]
+        slot = stat_in.at[spot(i // 2, i % 2)]
+        copy(stat_own, slot, s4.at[i - 1], r4.at[i - 1], device(0, i // 2, i % 2)).wait_recv()
+    total = stat_in[0]
+    for i in range(1, 8):
+        total = total + stat_in[i]
     stat_mid[...] = total
-    away = []
     for dz in range(1, depth):
-        hop = copy(stat_mid, stat_far.at[dz - 1], s5.at[dz - 1], r5.at[dz - 1], device(dz, 0, 0))
-        hop.start()
-        away.append(hop)
+        away.append(copy(stat_mid, stat_far.at[z], s5.at[dz - 1], r5.at[dz - 1], device(dz, 0, 0)))
+        away[-1].start()
+    stat_far[z] = total
     for dz in range(1, depth):
-        away[dz - 1].wait_recv()
-        total = total + stat_far[dz - 1]
+        slot = stat_far.at[lax.rem(z + depth - dz, depth)]
+        copy(stat_mid, slot, s5.at[dz - 1], r5.at[dz - 1], device(dz, 0, 0)).wait_recv()
+    total = stat_far[0]
+    for at in range(1, depth):
+        total = total + stat_far[at]
     sums = jnp.sum(total, axis=1, keepdims=True)
     factor = jnp.zeros_like(update)
     for l in range(layers):
         ratio = jnp.sqrt(sums[l:l + 1] / (sums[layers + l:layers + l + 1] + norm_eps))
         factor = factor + member_ref[l] * ratio
-    scaled = factor * update
-    for j in range(pieces):
-        lanes = pl.ds(pl.multiple_of(me * entries + j * TILE, TILE), TILE)
-        step_ref[:, lanes] = scaled[j * count:(j + 1) * count].astype(step_ref.dtype)
+
+    def place(dz, scaled):
+        owner = device(dz, 0, 0, back=True)
+        for j in range(pieces):
+            lanes = pl.ds(pl.multiple_of(owner * entries + j * TILE, TILE), TILE)
+            step_ref[:, lanes] = scaled[j * count:(j + 1) * count].astype(step_ref.dtype)
 
     def chunk(dz, dq, dc):
         return step_ref.at[:, pl.ds(pl.multiple_of(device(dz, dq, dc, back=True) * entries, TILE), entries)]
 
-    started = near + away + [hop for hops in (first_hop, second_hop, third_hop) for hop in hops.values()]
+    started = near + away + list(ahead.values()) + [hop for hops in (first_hop, second_hop, third_hop) for hop in hops.values()]
 
     def forward(dz, dq, dc, to_z, to_q, to_c, send, there):
         block = chunk(dz, dq, dc)
@@ -279,7 +321,7 @@
     def arrived(dz, dq, dc):
         block = chunk(dz, dq, dc)
         at = (dz * 4 + dq) * 2 + dc
-        copy(block, block, sz.at[0], rg.at[at], device(0, 0, 1)).wait_recv()
+        copy(block, block, sc.at[0], rg.at[at], device(0, 0, 1)).wait_recv()
 
     def spread(dz):
         for dq in order[:3]:
@@ -288,15 +330,16 @@
     def hand_over(dz, dq):
         forward(dz, dq, 0, 0, 0, 1, sc.at[dz * 4 + dq], (dz * 4 + dq) * 2 + 1)
 
-    for dz in range(1, depth):
-        forward(0, 0, 0, dz, 0, 0, sz.at[dz - 1], dz * 8)
+    scaled = factor * update
+    place(0, scaled)
     spread(0)
     hand_over(0, 0)
-    rows_ref[0] = weights - learn_rate * scaled
     for dz in reach:
-        arrived(dz, 0, 0)
+        ahead[dz].wait_recv()
+        place(dz, factor * update_far[dz - 1])
         spread(dz)
         hand_over(dz, 0)
+    rows_ref[0] = weights - learn_rate * scaled
     for dz in [0] + reach:
         for dq in (1, 2, 3):
             arrived(dz, dq, 0)
@@ -340,14 +383,20 @@
     dma = pltpu.SemaphoreType.DMA
     new_memory, packed, state, member = pl.pallas_call(
         pack_kernel,
-        in_specs=[smem, smem, hbm, hbm] + [vmem] * 3,
-        out_specs=[hbm] + [vmem] * 3,
+        in_specs=[smem, smem] + [hbm] * 5,
+        out_specs=[hbm] * 2 + [vmem] * 2,
         out_shape=[
             jax.ShapeDtypeStruct(memory.shape, jnp.bfloat16),
             jax.ShapeDtypeStruct((n * lines, TILE), f32),
             jax.ShapeDtypeStruct((3, lines, TILE), f32),
             jax.ShapeDtypeStruct((layers, lines, TILE), f32)],
-        scratch_shapes=[pltpu.VMEM((slabs, TILE, width), jnp.bfloat16)] * 3 + [dma((slabs,))] * 3,
+        scratch_shapes=[pltpu.VMEM((slabs, TILE, width), jnp.bfloat16)] * 3 + [
+            pltpu.VMEM((count, TILE, TILE), jnp.bfloat16),
+            pltpu.VMEM((count, TILE, TILE), jnp.bfloat16),
+            pltpu.VMEM((n * lines, TILE), f32),
+            pltpu.VMEM((3,) + master.shape, f32),
+            pltpu.SMEM((slabs * tile_count,), f32),
+            dma((slabs,)), dma((slabs,)), dma((slabs,)), dma((2 * count,)), dma((3,)), dma((1,))],
         name="pack",
     )(layer_ids, block_ids, grads, memory, master, first_moment, second_moment)
     stat_rows = -(-2 * layers // 8) * 8
@@ -365,12 +414,14 @@
             pltpu.VMEM((depth - 1, lines, TILE), f32),
             pltpu.VMEM((depth - 1, lines, TILE), f32),
             pltpu.VMEM((stat_rows, TILE), f32),
-            pltpu.VMEM((7, stat_rows, TILE), f32),
+            pltpu.VMEM((8, stat_rows, TILE), f32),
             pltpu.VMEM((stat_rows, TILE), f32),
-            pltpu.VMEM((depth - 1, stat_rows, TILE), f32),
+            pltpu.VMEM((depth, stat_rows, TILE), f32),
+            pltpu.VMEM((lines, TILE), f32),
+            pltpu.VMEM((depth - 1, lines, TILE), f32),
             dma((1,)), dma((depth * 4,)), dma((depth * 4,)), dma((depth * 3,)), dma((depth * 3,)), dma((depth - 1,)), dma((depth - 1,)),
             dma((7,)), dma((7,)), dma((depth - 1,)), dma((depth - 1,)),
-            dma((depth - 1,)), dma((depth * 3,)), dma((depth * 4,)), dma((n,))],
+            dma((depth - 1,)), dma((depth - 1,)), dma((depth * 3,)), dma((depth * 4,)), dma((n,))],
         compiler_params=pltpu.CompilerParams(collective_id=0, has_side_effects=True),
         name="exchange",
     )(packed.reshape(depth, 4, 2, lines, TILE), state, member)

time: 48.4 us -> 42.6 us (0.88)
  Pallas kernels: 47.6 us -> 41.7 us
    pallas_call x1, Pallas kernels: 35.4 us -> 31.2 us  [on_device_kernels(): pl.pallas_call(functools.partial(exchange_kernel, n), out_shape=[jax.Shap...]
    pallas_call x1, Pallas kernels: 9.68 us -> 8 us  [on_device_kernels(): pl.pallas_call(pack_kernel, in_specs=[smem, smem] + [hbm] * 5, out_specs=...]
where the time goes in v3:
time: 42.6 us; the launch traced here: 42.4 us
  Pallas kernels  41.7 us (98%)
  between operations  0.65 us (2%)
    pallas_call x1, Pallas kernels, on_device_kernels(): pl.pallas_call(functools.partial(exchange_kernel, n), out_shape=[jax.Shap...  31.2 us
    pallas_call x1, Pallas kernels, on_device_kernels(): pl.pallas_call(pack_kernel, in_specs=[smem, smem] + [hbm] * 5, out_specs=...  8 us
    pallas_call x1, Pallas kernels, on_device_kernels(): pl.pallas_call(functools.partial(state_kernel, layer_rows=tile_count * ti...  2.47 us

profile of v3, /device:TPU:0, one launch (start us, length us, event | category | flops | bytes accessed | tf_op | source)
XLA Modules:
  0.0 42.4 jit_solution(14399150457470789642)
XLA Ops:
  0.6 8.0 %pack.1 = (bf16[2,1024,1024]{2,1,0:T(8,128)(2,1)}, f32[2048,128]{1,0:T(8,128)}, f32[3,64,128]{2,1,0:T(8,128)}, f32[2,64,128]{2,1,0:T(8,128)}) custom-call(s32[16]{0:T(128)} %layers_smem.3, s32[16]{0:T(128)} %blocks_smem.3, bf16[2,1024,1024]{2,1,0:T(8,128)(2,1)} %grads_hbm.1, bf16[2,1024,1024]{2,1,0:T(8,128)(2,1)} %memory_hbm.1, f32[128,512]{1,0:T(8,128)} %master_ref.1, ...), custom_call_target="tpu_custom_call" | custom-call | tf_op jit(solution)/shard_map/pack/pallas_call | solution.py:384
  8.6 31.2 %exchange.1 = (f32[3,64,128]{2,1,0:T(8,128)}, bf16[16,16384]{1,0:T(8,128)(2,1)}) custom-call(f32[4,4,2,64,128]{4,3,2,1,0:T(8,128)} %bitcast.1, f32[3,64,128]{2,1,0:T(8,128)} %get-tuple-element.17.state_ref, f32[2,64,128]{2,1,0:T(8,128)} %get-tuple-element.18.member_ref), custom_call_target="tpu_custom_call" | custom-call | tf_op jit(solution)/shard_map/exchange/pallas_call | solution.py:403
  39.9 2.5 %state.1 = (f32[128,512]{1,0:T(8,128)}, f32[128,512]{1,0:T(8,128)}, f32[128,512]{1,0:T(8,128)}, bf16[16,16384]{1,0:T(8,128)(2,1)}) custom-call(s32[16]{0:T(128)} %layers_smem.3, s32[16]{0:T(128)} %blocks_smem.3, f32[3,64,128]{2,1,0:T(8,128)} %get-tuple-element.19.rows_ref, bf16[16,16384]{1,0:T(8,128)(2,1)} %get-tuple-element.20.step_ref, ...), custom_call_target="tpu_custom_call" | custom-call | tf_op jit(solution)/shard_map/state/pallas_call | solution.py:429

commit v4 on v3

--- a/solution.py
+++ b/solution.py
@@ -103,20 +103,14 @@
 
 
 def pack_kernel(layers_smem, blocks_smem, grads_hbm, memory_hbm, master_hbm, first_hbm, second_hbm,
-                out_hbm, packed_hbm, state_ref, member_ref,
-                grads_ref, memory_ref, out_ref, grad_tiles, memory_tiles, packed_ref, old_ref, rate_ref,
-                grads_sem, memory_sem, out_sem, tile_sem, old_sem, packed_sem):
+                packed_hbm, state_ref, member_ref, rate_ref,
+                grad_tiles, memory_tiles, packed_ref, old_ref, tile_sem, old_sem, packed_sem):
     count = layers_smem.shape[0]
     layers = member_ref.shape[0]
     pieces = state_ref.shape[1] // count
-    slabs = grads_ref.shape[0]
-    tile_count = slabs // layers
-
-    def moves(i):
-        layer, rows = lax.div(i, tile_count), pl.ds(pl.multiple_of(lax.rem(i, tile_count) * TILE, TILE), TILE)
-        return ((grads_hbm.at[layer, rows], grads_ref.at[i], grads_sem.at[i]),
-                (memory_hbm.at[layer, rows], memory_ref.at[i], memory_sem.at[i]),
-                (out_ref.at[i], out_hbm.at[layer, rows], out_sem.at[i]))
+    blocks = rate_ref.shape[0]
+    layer_tiles = blocks // layers
+    tile_count = grads_hbm.shape[1] // TILE
 
     tiles = []
     for k in range(count):
@@ -127,25 +121,19 @@
             tiles.append(pltpu.make_async_copy(
                 source.at[layers_smem[k], rows, lanes], held.at[k], tile_sem.at[s * count + k]))
             tiles[-1].start()
-
-    @pl.loop(0, slabs)
-    def _(i):
-        grads_in, memory_in, _ = moves(i)
-        pltpu.make_async_copy(*grads_in).start()
-        pltpu.make_async_copy(*memory_in).start()
-
     olds = []
     for s, source in enumerate((master_hbm, first_hbm, second_hbm)):
         olds.append(pltpu.make_async_copy(source, old_ref.at[s], old_sem.at[s]))
         olds[-1].start()
 
-    @pl.loop(0, slabs)
-    def _(i):
-        for t in range(tile_count):
-            rate_ref[i * tile_count + t] = jnp.float32(filter_rate)
-
+    for t in range(blocks):
+        rate_ref[t] = jnp.float32(filter_rate)
     for k in range(count):
-        rate_ref[layers_smem[k] * (tile_count * tile_count) + blocks_smem[k]] = jnp.float32(0.0)
+        rate_ref[layers_smem[k] * layer_tiles + blocks_smem[k]] = jnp.float32(0.0)
+        for l in range(layers):
+            flag = jnp.where(layers_smem[k] == l, jnp.float32(1.0), jnp.float32(0.0))
+            for j in range(pieces):
+                member_ref[l, j * count + k:j * count + k + 1, :] = jnp.full((1, TILE), flag, jnp.float32)
     for k in range(count):
         tiles[2 * k].wait()
         tiles[2 * k + 1].wait()
@@ -153,42 +141,21 @@
             grad_tiles[k].astype(jnp.float32) + memory_tiles[k].astype(jnp.float32))
     packed_out = pltpu.make_async_copy(packed_ref, packed_hbm, packed_sem.at[0])
     packed_out.start()
-
-    @pl.loop(0, slabs)
-    def _(i):
-        grads_in, memory_in, out = moves(i)
-        pltpu.make_async_copy(*grads_in).wait()
-        pltpu.make_async_copy(*memory_in).wait()
-        for t in range(tile_count):
-            lanes = slice(t * TILE, (t + 1) * TILE)
-            memory = memory_ref[i, :, lanes].astype(jnp.float32)
-            total = grads_ref[i, :, lanes].astype(jnp.float32) + memory
-            mixed = (1.0 - filter_rate) * memory + rate_ref[i * tile_count + t] * total
-            out_ref[i, :, lanes] = mixed.astype(out_ref.dtype)
-        pltpu.make_async_copy(*out).start()
-
     for old in olds:
         old.wait()
     for k in range(count):
-        column = layers_smem[k] * (tile_count * tile_count) + blocks_smem[k]
+        column = layers_smem[k] * layer_tiles + blocks_smem[k]
         for s in range(3):
             line = old_ref[s, pl.ds(column, 1), :]
             for j in range(pieces):
                 state_ref[s, j * count + k:j * count + k + 1, :] = line[:, j * TILE:(j + 1) * TILE]
-        for l in range(layers):
-            flag = jnp.where(layers_smem[k] == l, jnp.float32(1.0), jnp.float32(0.0))
-            for j in range(pieces):
-                member_ref[l, j * count + k:j * count + k + 1, :] = jnp.full((1, TILE), flag, jnp.float32)
     packed_out.wait()
 
-    @pl.loop(0, slabs)
-    def _(i):
-        pltpu.make_async_copy(*moves(i)[2]).wait()
-
-
-def exchange_kernel(n, packed_ref, state_ref, member_ref, rows_ref, step_ref,
-                    mine, recv1, send2, recv2, send3, recv3, stat_own, stat_in, stat_mid, stat_far, update_own, update_far,
-                    s0, s1, r1, s2, r2, s3, r3, s4, r4, s5, r5, sz, rz, sp, sc, rg):
+
+def exchange_kernel(n, packed_ref, state_ref, member_ref, rate_ref, grads_hbm, memory_hbm, rows_ref, step_ref, out_hbm,
+                    mine, recv1, send2, recv2, send3, recv3, stat_own, stat_in, stat_mid, stat_far, updates, grads_ref, memory_ref, out_ref,
+                    s0, s1, r1, s2, r2, s3, r3, s4, r4, s5, r5, sz, sp, ru, sc, rg,
+                    grads_sem, memory_sem, out_sem):
     depth = n // 8
     layers = member_ref.shape[0]
     count = step_ref.shape[0]
@@ -216,8 +183,38 @@
     peers = [device(0, i // 2, i % 2) for i in range(1, 8)] + [device(dz, 0, 0) for dz in range(1, depth)]
     for peer in peers:
         pl.semaphore_signal(barrier, inc=1, device_id=(peer,), device_id_type=pl.DeviceIdType.MESH)
+    slabs = grads_ref.shape[0]
+    tile_count = slabs // layers
+
+    def moves(i):
+        layer, rows = lax.div(i, tile_count), pl.ds(pl.multiple_of(lax.rem(i, tile_count) * TILE, TILE), TILE)
+        return ((grads_hbm.at[layer, rows], grads_ref.at[i], grads_sem.at[i]),
+                (memory_hbm.at[layer, rows], memory_ref.at[i], memory_sem.at[i]),
+                (out_ref.at[i], out_hbm.at[layer, rows], out_sem.at[i]))
+
+    def filter_slabs(start, stop):
+        @pl.loop(start, stop)
+        def _(i):
+            grads_in, memory_in, out = moves(i)
+            pltpu.make_async_copy(*grads_in).wait()
+            pltpu.make_async_copy(*memory_in).wait()
+            for t in range(tile_count):
+                lanes = slice(t * TILE, (t + 1) * TILE)
+                rate = rate_ref[i * tile_count + t]
+                mixed = (rate + (1.0 - filter_rate)) * memory_ref[i, :, lanes].astype(jnp.float32)
+                mixed = mixed + rate * grads_ref[i, :, lanes].astype(jnp.float32)
+                out_ref[i, :, lanes] = mixed.astype(out_ref.dtype)
+            pltpu.make_async_copy(*out).start()
+
     own_half = pltpu.make_async_copy(packed_ref.at[:, :, core], mine, s0.at[0])
     own_half.start()
+
+    @pl.loop(0, slabs)
+    def _(i):
+        grads_in, memory_in, _ = moves(i)
+        pltpu.make_async_copy(*grads_in).start()
+        pltpu.make_async_copy(*memory_in).start()
+
     weights = state_ref[0]
     stat_own[...] = jnp.zeros_like(stat_own)
     for l in range(layers):
@@ -242,6 +239,7 @@
             send2[place] = mine[at, plane(dq)] + recv1[slot]
             second_hop[place] = copy(send2.at[place], recv2.at[place], s2.at[place], r2.at[place], device(0, dq, 0))
             second_hop[place].start()
+    filter_slabs(0, slabs // 2)
     here = plane(0)
     summed = None
     for dz, at in targets:
@@ -255,6 +253,7 @@
             send3[dz - 1] = part
             third_hop[dz] = copy(send3.at[dz - 1], recv3.at[dz - 1], s3.at[dz - 1], r3.at[dz - 1], device(dz, 0, 0))
             third_hop[dz].start()
+    filter_slabs(slabs // 2, slabs - slabs // 4)
     for dz in range(1, depth):
         third_hop[dz].wait_recv()
         summed = summed + recv3[dz - 1]
@@ -273,10 +272,17 @@
     for i in range(1, 8):
         near.append(copy(stat_own, stat_in.at[spot(0, 0)], s4.at[i - 1], r4.at[i - 1], device(0, i // 2, i % 2)))
         near[-1].start()
-    update_own[...] = update
+    updates[0] = update
+
+    def lift(dz, dq, to_z, to_q, send, at):
+        hop = copy(updates.at[at], updates.at[dz * 4 + dq], send, ru.at[dz * 4 + dq], device(to_z, to_q, 0))
+        hop.start()
+        ahead[dz * 4 + dq] = hop
+
     for dz in range(1, depth):
-        ahead[dz] = copy(update_own, update_far.at[dz - 1], sz.at[dz - 1], rz.at[dz - 1], device(dz, 0, 0))
-        ahead[dz].start()
+        lift(dz, 0, dz, 0, sz.at[dz - 1], 0)
+    for dq in order[:3]:
+        lift(0, dq, 0, dq, sp.at[dq - 1], 0)
     stat_in[spot(0, 0)] = stat_own[...]
     for i in range(1, 8):
         slot = stat_in.at[spot(i // 2, i % 2)]
@@ -289,6 +295,11 @@
         away.append(copy(stat_mid, stat_far.at[z], s5.at[dz - 1], r5.at[dz - 1], device(dz, 0, 0)))
         away[-1].start()
     stat_far[z] = total
+    for dz in reach:
+        ahead[dz * 4].wait_recv()
+        for dq in order[:3]:
+            lift(dz, dq, 0, dq, sp.at[dz * 3 + dq - 1], dz * 4)
+    filter_slabs(slabs - slabs // 4, slabs)
     for dz in range(1, depth):
         slot = stat_far.at[lax.rem(z + depth - dz, depth)]
         copy(stat_mid, slot, s5.at[dz - 1], r5.at[dz - 1], device(dz, 0, 0)).wait_recv()
@@ -301,8 +312,9 @@
         ratio = jnp.sqrt(sums[l:l + 1] / (sums[layers + l:layers + l + 1] + norm_eps))
         factor = factor + member_ref[l] * ratio
 
-    def place(dz, scaled):
-        owner = device(dz, 0, 0, back=True)
+    def place(dz, dq):
+        scaled = factor * updates[dz * 4 + dq]
+        owner = device(dz, dq, 0, back=True)
         for j in range(pieces):
             lanes = pl.ds(pl.multiple_of(owner * entries + j * TILE, TILE), TILE)
             step_ref[:, lanes] = scaled[j * count:(j + 1) * count].astype(step_ref.dtype)
@@ -310,64 +322,85 @@
     def chunk(dz, dq, dc):
         return step_ref.at[:, pl.ds(pl.multiple_of(device(dz, dq, dc, back=True) * entries, TILE), entries)]
 
-    started = near + away + list(ahead.values()) + [hop for hops in (first_hop, second_hop, third_hop) for hop in hops.values()]
-
-    def forward(dz, dq, dc, to_z, to_q, to_c, send, there):
-        block = chunk(dz, dq, dc)
-        hop = copy(block, block, send, rg.at[there], device(to_z, to_q, to_c))
-        hop.start()
-        started.append(hop)
-
-    def arrived(dz, dq, dc):
-        block = chunk(dz, dq, dc)
-        at = (dz * 4 + dq) * 2 + dc
-        copy(block, block, sc.at[0], rg.at[at], device(0, 0, 1)).wait_recv()
-
-    def spread(dz):
-        for dq in order[:3]:
-            forward(dz, 0, 0, 0, dq, 0, sp.at[dz * 3 + dq - 1], (dz * 4 + dq) * 2)
-
-    def hand_over(dz, dq):
-        forward(dz, dq, 0, 0, 0, 1, sc.at[dz * 4 + dq], (dz * 4 + dq) * 2 + 1)
-
-    scaled = factor * update
-    place(0, scaled)
-    spread(0)
-    hand_over(0, 0)
-    for dz in reach:
-        ahead[dz].wait_recv()
-        place(dz, factor * update_far[dz - 1])
-        spread(dz)
-        hand_over(dz, 0)
-    rows_ref[0] = weights - learn_rate * scaled
-    for dz in [0] + reach:
-        for dq in (1, 2, 3):
-            arrived(dz, dq, 0)
-            hand_over(dz, dq)
-    for dz in range(depth):
-        for dq in range(4):
-            arrived(dz, dq, 1)
+    started = near + away + [
+        hop for hops in (ahead, first_hop, second_hop, third_hop) for hop in hops.values()]
+    reached = [0] + reach
+    for dz, dq in [(dz, 0) for dz in reached] + [(dz, dq) for dz in reached for dq in (1, 2, 3)]:
+        if dq:
+            ahead[dz * 4 + dq].wait_recv()
+        place(dz, dq)
+        block = chunk(dz, dq, 0)
+        started.append(copy(block, block, sc.at[dz * 4 + dq], rg.at[dz * 4 + dq], device(0, 0, 1)))
+        started[-1].start()
+    rows_ref[0] = weights - learn_rate * (factor * update)
+
+    @pl.loop(0, slabs)
+    def _(i):
+        pltpu.make_async_copy(*moves(i)[2]).wait()
+
+    for dz, dq in [(dz, dq) for dz in reached for dq in range(4)]:
+        block = chunk(dz, dq, 1)
+        copy(block, block, sc.at[dz * 4 + dq], rg.at[dz * 4 + dq], device(0, 0, 1)).wait_recv()
     for hop in started:
         hop.wait_send()
 
 
-def state_kernel(layers_smem, blocks_smem, rows_ref, step_ref, master_ref, first_ref, second_ref,
-                 master_out, first_out, second_out, step_out, *, layer_rows):
+def state_kernel(layers_smem, blocks_smem, rows_ref, step_hbm, kept_hbm, master_hbm, first_hbm, second_hbm,
+                 master_out, first_out, second_out, step_out, kept_out,
+                 old_ref, step_ref, kept_ref, in_sem, out_sem, slab_sem, *, layer_rows):
     count = layers_smem.shape[0]
     pieces = rows_ref.shape[1] // count
-    outs = ((master_ref, master_out), (first_ref, first_out), (second_ref, second_out))
-    step_out[...] = step_ref[...]
-    for old, new in outs:
-        new[...] = old[...]
-    for k in range(count):
-        column = layers_smem[k] * layer_rows + blocks_smem[k]
-        base = pl.ds(pl.multiple_of(lax.div(column, 8) * 8, 8), 8)
-        hit = lax.broadcasted_iota(jnp.int32, (8, TILE), 0) == lax.rem(column, 8)
-        for s, (_, new) in enumerate(outs):
+    slabs = kept_ref.shape[0]
+    tile_count = slabs // kept_hbm.shape[0]
+    olds, news = [], []
+    for s, (source, target) in enumerate(
+            ((master_hbm, master_out), (first_hbm, first_out), (second_hbm, second_out))):
+        olds.append(pltpu.make_async_copy(source, old_ref.at[s], in_sem.at[s]))
+        news.append(pltpu.make_async_copy(old_ref.at[s], target, out_sem.at[s]))
+    olds.append(pltpu.make_async_copy(step_hbm, step_ref, in_sem.at[3]))
+    news.append(pltpu.make_async_copy(step_ref, step_out, out_sem.at[3]))
+    for old in olds:
+        old.start()
+
+    def slab(i, hbm):
+        rows = pl.ds(pl.multiple_of(lax.rem(i, tile_count) * TILE, TILE), TILE)
+        return hbm.at[lax.div(i, tile_count), rows]
+
+    def coming(i):
+        return pltpu.make_async_copy(slab(i, kept_hbm), kept_ref.at[i], slab_sem.at[i])
+
+    def going(i):
+        return pltpu.make_async_copy(kept_ref.at[i], slab(i, kept_out), slab_sem.at[slabs + i])
+
+    @pl.loop(0, slabs)
+    def _(i):
+        coming(i).start()
+
+    for s in range(3):
+        olds[s].wait()
+        for k in range(count):
+            column = layers_smem[k] * layer_rows + blocks_smem[k]
+            base = pl.ds(pl.multiple_of(lax.div(column, 8) * 8, 8), 8)
+            hit = lax.broadcasted_iota(jnp.int32, (8, TILE), 0) == lax.rem(column, 8)
             for j in range(pieces):
                 lanes = slice(j * TILE, (j + 1) * TILE)
                 line = rows_ref[s, j * count + k:j * count + k + 1, :]
-                new[base, lanes] = jnp.where(hit, line, new[base, lanes])
+                old_ref[s, base, lanes] = jnp.where(hit, line, old_ref[s, base, lanes])
+        news[s].start()
+    olds[3].wait()
+    news[3].start()
+
+    @pl.loop(0, slabs)
+    def _(i):
+        coming(i).wait()
+        going(i).start()
+
+    @pl.loop(0, slabs)
+    def _(i):
+        going(i).wait()
+
+    for new in news:
+        new.wait()
 
 
 def on_device_kernels(n, grads, memory, block_ids, layer_ids, master, first_moment, second_moment):
@@ -381,31 +414,32 @@
     vmem, smem, hbm = (pl.BlockSpec(memory_space=m) for m in (pltpu.VMEM, pltpu.SMEM, pl.ANY))
     slabs = layers * tile_count
     dma = pltpu.SemaphoreType.DMA
-    new_memory, packed, state, member = pl.pallas_call(
+    slab = pltpu.VMEM((slabs, TILE, width), jnp.bfloat16)
+    packed, state, member, rates = pl.pallas_call(
         pack_kernel,
         in_specs=[smem, smem] + [hbm] * 5,
-        out_specs=[hbm] * 2 + [vmem] * 2,
+        out_specs=[hbm] + [vmem] * 2 + [smem],
         out_shape=[
-            jax.ShapeDtypeStruct(memory.shape, jnp.bfloat16),
             jax.ShapeDtypeStruct((n * lines, TILE), f32),
             jax.ShapeDtypeStruct((3, lines, TILE), f32),
-            jax.ShapeDtypeStruct((layers, lines, TILE), f32)],
-        scratch_shapes=[pltpu.VMEM((slabs, TILE, width), jnp.bfloat16)] * 3 + [
+            jax.ShapeDtypeStruct((layers, lines, TILE), f32),
+            jax.ShapeDtypeStruct((slabs * tile_count,), f32)],
+        scratch_shapes=[
             pltpu.VMEM((count, TILE, TILE), jnp.bfloat16),
             pltpu.VMEM((count, TILE, TILE), jnp.bfloat16),
             pltpu.VMEM((n * lines, TILE), f32),
             pltpu.VMEM((3,) + master.shape, f32),
-            pltpu.SMEM((slabs * tile_count,), f32),
-            dma((slabs,)), dma((slabs,)), dma((slabs,)), dma((2 * count,)), dma((3,)), dma((1,))],
+            dma((2 * count,)), dma((3,)), dma((1,))],
         name="pack",
     )(layer_ids, block_ids, grads, memory, master, first_moment, second_moment)
     stat_rows = -(-2 * layers // 8) * 8
-    rows, gathered = pl.pallas_call(
+    rows, gathered, kept = pl.pallas_call(
         functools.partial(exchange_kernel, n),
         out_shape=[jax.ShapeDtypeStruct((3, lines, TILE), f32),
-                   jax.ShapeDtypeStruct((count, n * entries), jnp.bfloat16)],
-        in_specs=[hbm, vmem, vmem],
-        out_specs=[vmem] * 2,
+                   jax.ShapeDtypeStruct((count, n * entries), jnp.bfloat16),
+                   jax.ShapeDtypeStruct(memory.shape, jnp.bfloat16)],
+        in_specs=[hbm, vmem, vmem, smem, hbm, hbm],
+        out_specs=[vmem, vmem, hbm],
         scratch_shapes=[
             pltpu.VMEM((depth, 4, lines, TILE), f32),
             pltpu.VMEM((depth * 4, lines, TILE), f32),
@@ -417,22 +451,26 @@
             pltpu.VMEM((8, stat_rows, TILE), f32),
             pltpu.VMEM((stat_rows, TILE), f32),
             pltpu.VMEM((depth, stat_rows, TILE), f32),
-            pltpu.VMEM((lines, TILE), f32),
-            pltpu.VMEM((depth - 1, lines, TILE), f32),
+            pltpu.VMEM((depth * 4, lines, TILE), f32),
+            slab, slab, slab,
             dma((1,)), dma((depth * 4,)), dma((depth * 4,)), dma((depth * 3,)), dma((depth * 3,)), dma((depth - 1,)), dma((depth - 1,)),
             dma((7,)), dma((7,)), dma((depth - 1,)), dma((depth - 1,)),
-            dma((depth - 1,)), dma((depth - 1,)), dma((depth * 3,)), dma((depth * 4,)), dma((n,))],
+            dma((depth - 1,)), dma((depth * 3,)), dma((depth * 4,)), dma((depth * 4,)), dma((depth * 4,)),
+            dma((slabs,)), dma((slabs,)), dma((slabs,))],
         compiler_params=pltpu.CompilerParams(collective_id=0, has_side_effects=True),
         name="exchange",
-    )(packed.reshape(depth, 4, 2, lines, TILE), state, member)
+    )(packed.reshape(depth, 4, 2, lines, TILE), state, member, rates, grads, memory)
     like = jax.ShapeDtypeStruct(master.shape, f32)
-    master_new, first_new, second_new, step_blocks = pl.pallas_call(
+    master_new, first_new, second_new, step_blocks, new_memory = pl.pallas_call(
         functools.partial(state_kernel, layer_rows=tile_count * tile_count),
-        out_shape=[like] * 3 + [jax.ShapeDtypeStruct(gathered.shape, jnp.bfloat16)],
-        in_specs=[smem, smem] + [vmem] * 5,
-        out_specs=[vmem] * 4,
+        out_shape=[like] * 3 + [jax.ShapeDtypeStruct(gathered.shape, jnp.bfloat16),
+                                jax.ShapeDtypeStruct(memory.shape, jnp.bfloat16)],
+        in_specs=[smem, smem, vmem] + [hbm] * 5,
+        out_specs=[hbm] * 5,
+        scratch_shapes=[pltpu.VMEM((3,) + master.shape, f32), pltpu.VMEM(gathered.shape, jnp.bfloat16), slab,
+                        dma((4,)), dma((4,)), dma((2 * slabs,))],
         name="state",
-    )(layer_ids, block_ids, rows, gathered, master, first_moment, second_moment)
+    )(layer_ids, block_ids, rows, gathered, kept, master, first_moment, second_moment)
     return (new_memory, master_new, first_new, second_new, step_blocks)
 
 

time: 42.6 us -> 42.2 us (level)
    pallas_call x1, Pallas kernels: 8 us -> 4.04 us  [on_device_kernels(): pl.pallas_call(pack_kernel, in_specs=[smem, smem] + [hbm] * 5, out_specs=...]
    pallas_call x1, Pallas kernels: 2.47 us -> 6.05 us  [on_device_kernels(): pl.pallas_call(functools.partial(state_kernel, layer_rows=tile_count * ti...]
where the time goes in v4:
time: 42.2 us; the launch traced here: 41.9 us
  Pallas kernels  41.3 us (98%)
  between operations  0.65 us (2%)
    pallas_call x1, Pallas kernels, on_device_kernels(): pl.pallas_call(functools.partial(exchange_kernel, n), out_shape=[jax.Shap...  31.2 us
    pallas_call x1, Pallas kernels, on_device_kernels(): pl.pallas_call(functools.partial(state_kernel, layer_rows=tile_count * ti...  6.05 us
    pallas_call x1, Pallas kernels, on_device_kernels(): pl.pallas_call(pack_kernel, in_specs=[smem, smem] + [hbm] * 5, out_specs=...  4.04 us

profile of v4, /device:TPU:0, one launch (start us, length us, event | category | flops | bytes accessed | tf_op | source)
XLA Modules:
  0.0 41.9 jit_solution(2795627044531762483)
XLA Ops:
  0.6 4.0 %pack.1 = (f32[2048,128]{1,0:T(8,128)}, f32[3,64,128]{2,1,0:T(8,128)}, f32[2,64,128]{2,1,0:T(8,128)}, f32[128]{0:T(128)}) custom-call(s32[16]{0:T(128)} %layers_smem.3, s32[16]{0:T(128)} %blocks_smem.3, bf16[2,1024,1024]{2,1,0:T(8,128)(2,1)} %grads_hbm.3, bf16[2,1024,1024]{2,1,0:T(8,128)(2,1)} %memory_hbm.3, f32[128,512]{1,0:T(8,128)} %master_hbm.3, ...), custom_call_target="tpu_custom_call" | custom-call | tf_op jit(solution)/shard_map/pack/pallas_call | solution.py:418
  4.7 31.2 %exchange.1 = (f32[3,64,128]{2,1,0:T(8,128)}, bf16[16,16384]{1,0:T(8,128)(2,1)}, bf16[2,1024,1024]{2,1,0:T(8,128)(2,1)}) custom-call(f32[4,4,2,64,128]{4,3,2,1,0:T(8,128)} %bitcast.1, f32[3,64,128]{2,1,0:T(8,128)} %get-tuple-element.18.state_ref, f32[2,64,128]{2,1,0:T(8,128)} %get-tuple-element.19.member_ref, f32[128]{0:T(128)} %get-tuple-element.20.rate_ref, ...), custom_call_target="tpu_custom_call" | custom-call | tf_op jit(solution)/shard_map/exchange/pallas_call | solution.py:436
  35.9 6.0 %state.1 = (f32[128,512]{1,0:T(8,128)}, f32[128,512]{1,0:T(8,128)}, f32[128,512]{1,0:T(8,128)}, bf16[16,16384]{1,0:T(8,128)(2,1)}, bf16[2,1024,1024]{2,1,0:T(8,128)(2,1)}) custom-call(s32[16]{0:T(128)} %layers_smem.3, s32[16]{0:T(128)} %blocks_smem.3, f32[3,64,128]{2,1,0:T(8,128)} %get-tuple-element.21.rows_ref, ...), custom_call_target="tpu_custom_call" | custom-call | tf_op jit(solution)/shard_map/state/pallas_call | solution.py:464

commit v5 on v4

--- a/solution.py
+++ b/solution.py
@@ -208,13 +208,6 @@
 
     own_half = pltpu.make_async_copy(packed_ref.at[:, :, core], mine, s0.at[0])
     own_half.start()
-
-    @pl.loop(0, slabs)
-    def _(i):
-        grads_in, memory_in, _ = moves(i)
-        pltpu.make_async_copy(*grads_in).start()
-        pltpu.make_async_copy(*memory_in).start()
-
     weights = state_ref[0]
     stat_own[...] = jnp.zeros_like(stat_own)
     for l in range(layers):
@@ -232,6 +225,13 @@
                                    s1.at[slot], r1.at[slot], device(0, 0, 1))
             first_hop[slot].start()
     own_half.wait()
+
+    @pl.loop(0, slabs)
+    def _(i):
+        grads_in, memory_in, _ = moves(i)
+        pltpu.make_async_copy(*grads_in).start()
+        pltpu.make_async_copy(*memory_in).start()
+
     for dz, at in targets:
         for dq in order[:3]:
             slot, place = dz * 4 + dq, dz * 3 + dq - 1

time: 42.2 us -> 42.2 us (level)
  no operation moved by 1% of the time
where the time goes in v5:
time: 42.2 us; the launch traced here: 41.9 us
  Pallas kernels  41.3 us (98%)
  between operations  0.65 us (2%)
    pallas_call x1, Pallas kernels, on_device_kernels(): pl.pallas_call(functools.partial(exchange_kernel, n), out_shape=[jax.Shap...  31.2 us
    pallas_call x1, Pallas kernels, on_device_kernels(): pl.pallas_call(functools.partial(state_kernel, layer_rows=tile_count * ti...  6.05 us
    pallas_call x1, Pallas kernels, on_device_kernels(): pl.pallas_call(pack_kernel, in_specs=[smem, smem] + [hbm] * 5, out_specs=...  4.04 us

profile of v5, /device:TPU:0, one launch (start us, length us, event | category | flops | bytes accessed | tf_op | source)
XLA Modules:
  0.0 41.9 jit_solution(3731217725449748119)
XLA Ops:
  0.6 4.0 %pack.1 = (f32[2048,128]{1,0:T(8,128)}, f32[3,64,128]{2,1,0:T(8,128)}, f32[2,64,128]{2,1,0:T(8,128)}, f32[128]{0:T(128)}) custom-call(s32[16]{0:T(128)} %layers_smem.3, s32[16]{0:T(128)} %blocks_smem.3, bf16[2,1024,1024]{2,1,0:T(8,128)(2,1)} %grads_hbm.3, bf16[2,1024,1024]{2,1,0:T(8,128)(2,1)} %memory_hbm.3, f32[128,512]{1,0:T(8,128)} %master_hbm.3, ...), custom_call_target="tpu_custom_call" | custom-call | tf_op jit(solution)/shard_map/pack/pallas_call | solution.py:418
  4.7 31.2 %exchange.1 = (f32[3,64,128]{2,1,0:T(8,128)}, bf16[16,16384]{1,0:T(8,128)(2,1)}, bf16[2,1024,1024]{2,1,0:T(8,128)(2,1)}) custom-call(f32[4,4,2,64,128]{4,3,2,1,0:T(8,128)} %bitcast.1, f32[3,64,128]{2,1,0:T(8,128)} %get-tuple-element.18.state_ref, f32[2,64,128]{2,1,0:T(8,128)} %get-tuple-element.19.member_ref, f32[128]{0:T(128)} %get-tuple-element.20.rate_ref, ...), custom_call_target="tpu_custom_call" | custom-call | tf_op jit(solution)/shard_map/exchange/pallas_call | solution.py:436
  35.9 6.0 %state.1 = (f32[128,512]{1,0:T(8,128)}, f32[128,512]{1,0:T(8,128)}, f32[128,512]{1,0:T(8,128)}, bf16[16,16384]{1,0:T(8,128)(2,1)}, bf16[2,1024,1024]{2,1,0:T(8,128)(2,1)}) custom-call(s32[16]{0:T(128)} %layers_smem.3, s32[16]{0:T(128)} %blocks_smem.3, f32[3,64,128]{2,1,0:T(8,128)} %get-tuple-element.21.rows_ref, ...), custom_call_target="tpu_custom_call" | custom-call | tf_op jit(solution)/shard_map/state/pallas_call | solution.py:464
